TPU v7x, 512 devices: a whole 4x8x8 slice. The times are simulated.
512 devices in a mesh: dom: 64 (over z_lo, x, y), snap: 8 (over z_hi, core).
Axes of the slice: x: 4, y: 8, z: 8 (z_hi: 4, z_lo: 2; z = z_hi * 2 + z_lo), core: 2. Of those that a mesh axis runs over, the one named last changes fastest.
Arguments:
- features: bfloat16 [8, 8192, 256], P('snap', 'dom'), may hold values from -6 to 6
- cotangent: bfloat16 [8, 8192, 256], P('snap', 'dom'), may hold values from -6 to 6
- neighbours: int32 [8192, 16], P('dom'), may hold values from 0 to 8191, as said below
- degrees: int32 [8192], P('dom'), may hold values from 1 to 16
- message_proj: bfloat16 [256, 256], replicated, may hold values from -0.375 to 0.375
- combine_proj: bfloat16 [256, 256], replicated, may hold values from -0.375 to 0.375
- attend_proj: bfloat16 [256, 768], replicated, may hold values from -0.375 to 0.375
- output_proj: bfloat16 [256, 256], replicated, may hold values from -0.375 to 0.375
Outputs:
- grad_features: bfloat16 [8, 8192, 256], P('snap', 'dom')
- grad_message: float32 [256, 256], replicated
- grad_combine: float32 [256, 256], replicated
- grad_attend: float32 [256, 768], replicated
- grad_output: float32 [256, 256], replicated
Inputs may be any that keep to these rules, and one draw needn't show every extreme that they name: `neighbours`: a neighbour of a node in rows p * 128 to (p + 1) * 128 - 1 lies in rows p * 128 - 128 to (p + 1) * 128 + 127; slot 0 of the first and of the second node of such a block names the lowest and the highest of those rows that exist.
All inputs are finite; a program needn't handle non-finite values.
Results may differ from a plain program's by a relative error of at most 0.012.
Values may be sent and summed in bfloat16 or wider, within the bound.
No kernel may reach another device: no remote copies, remote signals or barrier semaphores. Data moves between devices by JAX's collectives and lax.ppermute only.
A program may use at most 64 MiB of HBM per device.

v0:
```python
import math

import jax
import jax.numpy as jnp
from jax import lax
from jax.sharding import PartitionSpec as P

HEAD_DIM = 32
SNAPS = 8
HALO = 128


def with_halo(cells, sides, width):
    for axis, dim in sides:
        count = lax.axis_size(axis)
        ends = count - 1
        head = lax.slice_in_dim(cells, 0, width, axis=dim)
        tail = lax.slice_in_dim(cells, cells.shape[dim] - width, cells.shape[dim], axis=dim)
        cells = jnp.concatenate(
            [
                lax.ppermute(tail, axis, [(i, (i + 1) % count) for i in range(ends)]),
                cells,
                lax.ppermute(head, axis, [((i + 1) % count, i) for i in range(ends)]),
            ],
            axis=dim,
        )
    return cells


def in_one_piece(arrays, axis, split_dim, concat_dim, along):
    both = jnp.concatenate(arrays, axis=along)
    filled, at, gathered = (
        lax.all_to_all(both, axis, split_axis=split_dim, concat_axis=concat_dim, tiled=True),
        0,
        [],
    )
    for a in arrays:
        gathered.append(lax.slice_in_dim(filled, at, at + a.shape[along], axis=along))
        at += a.shape[along]
    return tuple(gathered)


def in_one(arrays, axis):
    line, at, gathered = (jnp.concatenate([a.reshape(-1) for a in arrays]), 0, [])
    subtotal = lax.psum(line, axis)
    for a in arrays:
        gathered.append(subtotal[at : at + a.size].reshape(a.shape))
        at += a.size
    return tuple(gathered)


def silu_slope(inputs_pre):
    logistic = jax.nn.sigmoid(inputs_pre)
    return logistic * (1.0 + inputs_pre * (1.0 - logistic))


def edge_inputs(message_rows, own_block, neighbour_block, degree_block):
    gathered = jnp.take(message_rows, neighbour_block, axis=0)
    before = gathered + own_block.astype(jnp.float32)[:, None, :]
    slot_index = jnp.arange(neighbour_block.shape[1], dtype=jnp.int32)
    used = (slot_index[None, :] < degree_block[:, None]).astype(jnp.float32)
    weights = used / degree_block.astype(jnp.float32)[:, None]
    return (before, weights)


def spatial_forward(own_rows, message_rows, neighbour_index, degrees, combine_proj, block_rows):
    node_count = own_rows.shape[0]

    def per_block(block_index):
        before, weights = edge_inputs(message_rows, own_rows, neighbour_index, degrees)
        return jnp.sum(jax.nn.silu(before) * weights[:, :, None], axis=1)

    combined = lax.map(per_block, jnp.arange(node_count // block_rows, dtype=jnp.int32))
    combined = combined.reshape(node_count, -1).astype(jnp.bfloat16)
    spatial = own_rows.astype(jnp.float32) + jnp.dot(
        combined, combine_proj, preferred_element_type=jnp.float32
    )
    return (combined, spatial.astype(jnp.bfloat16))


def spatial_backward(
    own_rows, message_rows, neighbour_index, degrees, grad_spatial, combine_proj, block_rows
):
    node_count = own_rows.shape[0]
    feature_width = own_rows.shape[1]
    grad_combined = jnp.dot(grad_spatial, combine_proj.T, preferred_element_type=jnp.float32)

    def per_block(totals, block_index):
        before, weights = edge_inputs(message_rows, own_rows, neighbour_index, degrees)
        grad_before = grad_combined[:, None, :] * weights[:, :, None] * silu_slope(before)
        totals = totals.at[neighbour_index.reshape(-1)].add(grad_before.reshape(-1, feature_width))
        return (totals, jnp.sum(grad_before, axis=1))

    start_rows = jnp.zeros((message_rows.shape[0], feature_width), jnp.float32)
    grad_rows, self_terms = lax.scan(
        per_block, start_rows, jnp.arange(node_count // block_rows, dtype=jnp.int32)
    )
    return (grad_rows, self_terms.reshape(node_count, feature_width))


def temporal_block(spat_block, cot_block, attend_proj, output_proj):
    snap_count, node_count, feature_width = spat_block.shape
    head_count = feature_width // HEAD_DIM
    row_count = snap_count * node_count
    flat_spat = spat_block.reshape(row_count, feature_width)
    flat_cot = cot_block.reshape(row_count, feature_width)
    projected = jnp.dot(flat_spat, attend_proj, preferred_element_type=jnp.float32)
    projected = projected.reshape(snap_count, node_count, 3, head_count, HEAD_DIM)
    query_rows = projected[:, :, 0]
    key_rows = projected[:, :, 1]
    value_rows = projected[:, :, 2]
    inverse_root = 1.0 / math.sqrt(HEAD_DIM)
    precise = lax.Precision.HIGHEST
    scores = jnp.einsum("snhe,rnhe->nhsr", query_rows, key_rows, precision=precise) * inverse_root
    exponent = jnp.exp(scores)
    soft_weights = exponent / jnp.sum(exponent, axis=-1, keepdims=True)
    attended = jnp.einsum("nhsr,rnhe->snhe", soft_weights, value_rows, precision=precise)
    attended = attended.reshape(row_count, feature_width).astype(jnp.bfloat16)
    grad_output = jnp.dot(attended.T, flat_cot, preferred_element_type=jnp.float32)
    grad_attended = jnp.dot(flat_cot, output_proj.T, preferred_element_type=jnp.float32)
    grad_attended = grad_attended.reshape(snap_count, node_count, head_count, HEAD_DIM)
    grad_soft = jnp.einsum("snhe,rnhe->nhsr", grad_attended, value_rows, precision=precise)
    grad_value = jnp.einsum("nhsr,snhe->rnhe", soft_weights, grad_attended, precision=precise)
    grad_score = (
        soft_weights
        * (grad_soft - jnp.sum(soft_weights * grad_soft, axis=-1, keepdims=True))
        * inverse_root
    )
    grad_query = jnp.einsum("nhsr,rnhe->snhe", grad_score, key_rows, precision=precise)
    grad_key = jnp.einsum("nhsr,snhe->rnhe", grad_score, query_rows, precision=precise)
    grad_three = jnp.stack([grad_query, grad_key, grad_value], axis=2)
    grad_three = grad_three.reshape(row_count, 3 * feature_width).astype(jnp.bfloat16)
    grad_attend = jnp.dot(flat_spat.T, grad_three, preferred_element_type=jnp.float32)
    grad_spatial = flat_cot.astype(jnp.float32) + jnp.dot(
        grad_three, attend_proj.T, preferred_element_type=jnp.float32
    )
    grad_spatial = grad_spatial.astype(jnp.bfloat16).reshape(snap_count, node_count, feature_width)
    return (grad_spatial, grad_attend, grad_output)


def body(
    features, cotangent, neighbours, degrees, message_proj, combine_proj, attend_proj, output_proj
):
    local_count, node_count, feature_width = features.shape
    block_rows = min(256, node_count)
    first_row = lax.axis_index("dom") * node_count - HALO
    neighbour_local = neighbours - first_row
    extended = with_halo(features, (("dom", 1),), HALO)
    snapshot = 0
    message_rows = jnp.dot(extended[snapshot], message_proj, preferred_element_type=jnp.float32)
    combined, spatial = spatial_forward(
        features[snapshot], message_rows, neighbour_local, degrees, combine_proj, block_rows
    )
    message_list = [message_rows]
    combined_list = [combined]
    spatial_list = [spatial]
    spatial_all = jnp.stack(spatial_list)
    spat_swapped, cot_swapped = in_one_piece((spatial_all, cotangent), "snap", 1, 0, 2)
    snap_count = spat_swapped.shape[0]
    node_share = spat_swapped.shape[1]
    node_block = min(128, node_share)

    def temporal_step(totals, block_index):
        grad_block, grad_attend, grad_output = temporal_block(
            spat_swapped, cot_swapped, attend_proj, output_proj
        )
        return ((totals[0] + grad_attend, totals[1] + grad_output, grad_block), None)

    start_totals = (
        jnp.zeros((feature_width, 3 * feature_width), jnp.float32),
        jnp.zeros((feature_width, feature_width), jnp.float32),
        jnp.zeros((snap_count, node_share, feature_width), jnp.bfloat16),
    )
    totals, unused_out = lax.scan(
        temporal_step, start_totals, jnp.arange(node_share // node_block, dtype=jnp.int32)
    )
    raw_attend, raw_output, grad_swapped = totals
    raw_attend, raw_output = lax.psum((raw_attend, raw_output), ("dom", "snap"))
    grad_spatial_all = lax.all_to_all(grad_swapped, "snap", split_axis=0, concat_axis=1, tiled=True)
    snapshot = 0
    grad_spatial = grad_spatial_all[snapshot]
    raw_combine = jnp.dot(
        combined_list[snapshot].T, grad_spatial, preferred_element_type=jnp.float32
    )
    grad_rows, self_terms = spatial_backward(
        features[snapshot],
        message_list[snapshot],
        neighbour_local,
        degrees,
        grad_spatial,
        combine_proj,
        block_rows,
    )
    grad_row_list = [grad_rows]
    self_list = [self_terms]
    ghost_list = [jnp.concatenate([grad_rows[:HALO], grad_rows[node_count + HALO :]], axis=0)]
    returned = with_halo(jnp.stack(ghost_list).astype(jnp.bfloat16), (("dom", 1),), HALO).astype(
        jnp.float32
    )
    snapshot = 0
    own_grads = grad_row_list[snapshot][HALO : HALO + node_count]
    own_grads = own_grads.at[:HALO].add(returned[snapshot, :HALO])
    own_grads = own_grads.at[node_count - HALO :].add(returned[snapshot, 3 * HALO :])
    own_grads = own_grads.astype(jnp.bfloat16)
    raw_message = jnp.dot(features[snapshot].T, own_grads, preferred_element_type=jnp.float32)
    grad_here = grad_spatial_all[snapshot].astype(jnp.float32) + self_list[snapshot]
    grad_here = grad_here + jnp.dot(own_grads, message_proj.T, preferred_element_type=jnp.float32)
    grad_list = [grad_here.astype(jnp.bfloat16)]
    grad_features = jnp.stack(grad_list)
    raw_message, raw_combine = in_one((raw_message, raw_combine), ("dom", "snap"))
    factor = 1.0 / math.sqrt(SNAPS * lax.axis_size("dom") * node_count)
    return (
        grad_features,
        raw_message * factor,
        raw_combine * factor,
        raw_attend * factor,
        raw_output * factor,
    )


def solution(mesh):
    in_specs = (
        P("snap", "dom", None),
        P("snap", "dom", None),
        P("dom", None),
        P("dom"),
        P(),
        P(),
        P(),
        P(),
    )
    out_specs = (P("snap", "dom", None), P(), P(), P(), P())
    return jax.shard_map(body, mesh=mesh, in_specs=in_specs, out_specs=out_specs, check_vma=False)
```

profile of v0, /device:TPU:17, one launch (start us, length us, event | category | flops | bytes accessed | tf_op | source)
XLA Modules:
  0.0 398.8 jit_solution(7515631728023521003)
XLA Ops:
  7.2 3.3 collective-permute-start
  10.5 2.1 collective-permute-start.1
  12.6 0.9 bitcast_convert_fusion
  16.1 1.2 copy.82
  17.3 1.0 fusion.16
  18.4 6.6 %gather_fusion = f32[2048,256]{1,0:T(8,128)S(1)} fusion(f32[384,256]{1,0:T(8,128)S(1)} %fusion.16, s32[2048]{0:T(1024)S(1)} %broadcast_clamp_fusion), kind=kCustom, calls=%fused_computation.clone | custom fusion | bytes 4202496 | tf_op jit(solution)/shard_map/while/body/eval_jaxpr/jit(_take)/gather | solution.py:58
  25.1 1.2 multiply_reduce_fusion
  27.2 1.4 reduce.6
  29.4 11.6 %all-to-all-start = ((bf16[8,2,4096]{2,1,0:T(2,128)(2,1)}), bf16[8,2,4096]{2,1,0:T(2,128)(2,1)S(1)}, u32[]{:S(2)}, u32[]{:S(2)}) async-start(bf16[8,2,4096]{2,1,0:T(2,128)(2,1)} %reshape.353), calls=%async_computation | async-start | bytes 262144 | tf_op jit(solution)/shard_map/all_to_all | solution.py:33
  41.6 8.1 %all-to-all-done = bf16[8,2,4096]{2,1,0:T(2,128)(2,1)S(1)} async-done(((bf16[8,2,4096]{2,1,0:T(2,128)(2,1)}), bf16[8,2,4096]{2,1,0:T(2,128)(2,1)S(1)}, u32[]{:S(2)}, u32[]{:S(2)}) %all-to-all-start) | async-done | bytes 131104 | tf_op jit(solution)/shard_map/all_to_all | solution.py:33
  51.7 1.2 fusion.10
  52.9 1.6 fusion
  54.5 3.8 multiply_reduce_fusion.1
  58.3 2.1 fusion.1
  60.4 1.0 convolution_bitcast_fusion
  61.3 1.3 convolution_bitcast_fusion.1
  62.6 1.4 convolution_bitcast_fusion.2
  64.9 1.0 copy.96
  66.1 1.9 fusion.2
  68.0 4.5 %all-to-all-start.1 = ((bf16[8,16,256]{2,1,0:T(8,128)(2,1)}), bf16[8,16,256]{2,1,0:T(8,128)(2,1)S(1)}, u32[]{:S(2)}, u32[]{:S(2)}) async-start(bf16[8,16,256]{2,1,0:T(8,128)(2,1)} %bitcast.22), calls=%async_computation.1 | async-start | bytes 131072 | tf_op jit(solution)/shard_map/all_to_all | solution.py:179
  72.5 2.0 fusion.41
  74.5 0.9 fusion.42
  75.4 4.4 %all-to-all-done.1 = bf16[8,16,256]{2,1,0:T(8,128)(2,1)S(1)} async-done(((bf16[8,16,256]{2,1,0:T(8,128)(2,1)}), bf16[8,16,256]{2,1,0:T(8,128)(2,1)S(1)}, u32[]{:S(2)}, u32[]{:S(2)}) %all-to-all-start.1) | async-done | bytes 65568 | tf_op jit(solution)/shard_map/all_to_all | solution.py:179
  80.2 2.8 fusion.37
  83.0 12.1 %scatter_custom_fusion = f32[384,256]{1,0:T(8,128)S(1)} fusion(s32[2048]{0:T(1024)} %bitcast.128, f32[2048,256]{1,0:T(8,128)} %bitcast.110, f32[]{:T(128)} %constant.129.clone.1), kind=kCustom, calls=%fused_computation.48 | custom fusion | flops 524288 | bytes 393728 | tf_op jit(solution)/shard_map/while/body/eval_jaxpr/scatter-add | solution.py:91
  95.1 2.0 collective-permute-start.3
  97.2 4.8 %collective-permute-start.2 = (bf16[1,128,256]{2,1,0:T(8,128)(2,1)S(1)}, bf16[1,128,256]{2,1,0:T(8,128)(2,1)S(1)}, u32[]{:S(2)}, u32[]{:S(2)}) collective-permute-start(bf16[1,128,256]{2,1,0:T(8,128)(2,1)S(1)} %bitcast.125), channel_id=1, source_target_pairs={{0,8},{8,16},{16,24},{24,32},{32,40},{40,48},{48,56},{56,64},{64,7... | collective-permute-start | bytes 196616 | tf_op jit(solution)/shard_map/ppermute | solution.py:21
  102.1 1.1 collective-permute-done.2
  104.6 0.8 fusion.5
  105.4 282.2 %all-reduce.3.cloned.1.call-done = (f32[131072]{0:T(1024)}, f32[256,768]{1,0:T(8,128)}, f32[256,256]{1,0:T(8,128)}) async-done(((f32[131072]{0:T(1024)}, f32[256,768]{1,0:T(8,128)}, f32[256,256]{1,0:T(8,128)}), (f32[131072]{0:T(1024)}, f32[256,768]{1,0:T(8,128)}, f32[256,256]{1,0:T(8,128)})) %all-reduce.3.cloned.1.call-update) | async-done | bytes 1572880 | tf_op jit(solution)/shard_map/psum | solution.py:45
  387.6 1.2 slice_multiply_fusion
  391.1 0.9 broadcast_multiply_fusion
  (63 shorter events, 12.0 us)
Async XLA Ops:
  7.2 10.2 %copy-start = (bf16[256,256]{1,0:T(8,128)(2,1)S(1)}, bf16[256,256]{1,0:T(8,128)(2,1)}, u32[]{:S(2)}) copy-start(bf16[256,256]{1,0:T(8,128)(2,1)} %param.22) | copy-start | bytes 393220
  7.2 10.1 %collective-permute-start = (bf16[1,128,256]{2,1,0:T(8,128)(2,1)}, bf16[1,128,256]{2,1,0:T(8,128)(2,1)S(1)}, u32[]{:S(2)}, u32[]{:S(2)}) collective-permute-start(bf16[1,128,256]{2,1,0:T(8,128)(2,1)} %param.18), channel_id=1, source_target_pairs={{0,8},{8,16},{16,24},{24,32},{32,40},{40,48},{48,56},{56,64},{64,7... | collective-permute-start | bytes 196616 | tf_op jit(solution)/shard_map/ppermute | solution.py:21
  10.5 6.8 %collective-permute-start.1 = (bf16[1,128,256]{2,1,0:T(8,128)(2,1)}, bf16[1,128,256]{2,1,0:T(8,128)(2,1)S(1)}, u32[]{:S(2)}, u32[]{:S(2)}) collective-permute-start(bf16[1,128,256]{2,1,0:T(8,128)(2,1)} %param.18), channel_id=1, source_target_pairs={{8,0},{16,8},{24,16},{32,24},{40,32},{48,40},{56,48},{64,56},{72,6... | collective-permute-start | bytes 196616 | tf_op jit(solution)/shard_map/ppermute | solution.py:23
  25.0 1.3 copy-start.1
  25.0 1.3 copy-start.4
  25.1 1.4 copy-start.8
  29.4 20.3 %all-to-all-start = ((bf16[8,2,4096]{2,1,0:T(2,128)(2,1)}), bf16[8,2,4096]{2,1,0:T(2,128)(2,1)S(1)}, u32[]{:S(2)}, u32[]{:S(2)}) async-start(bf16[8,2,4096]{2,1,0:T(2,128)(2,1)} %reshape.353), calls=%async_computation | async-start | bytes 262144 | tf_op jit(solution)/shard_map/all_to_all | solution.py:33
  50.5 0.9 copy-start.7
  64.8 9.6 %copy-start.3 = (bf16[8,16,256]{2,1,0:T(8,128)(2,1)S(1)}, bf16[8,16,256]{2,1,0:T(8,128)(2,1)}, u32[]{:S(2)}) copy-start(bf16[8,16,256]{2,1,0:T(8,128)(2,1)} %get-tuple-element.127) | copy-start | bytes 196612
  64.9 14.9 %copy-start.5 = (bf16[256,256]{1,0:T(8,128)(2,1)S(1)}, bf16[256,256]{1,0:T(8,128)(2,1)}, u32[]{:S(2)}) copy-start(bf16[256,256]{1,0:T(8,128)(2,1)} %param.23) | copy-start | bytes 393220
  68.0 11.8 %all-to-all-start.1 = ((bf16[8,16,256]{2,1,0:T(8,128)(2,1)}), bf16[8,16,256]{2,1,0:T(8,128)(2,1)S(1)}, u32[]{:S(2)}, u32[]{:S(2)}) async-start(bf16[8,16,256]{2,1,0:T(8,128)(2,1)} %bitcast.22), calls=%async_computation.1 | async-start | bytes 131072 | tf_op jit(solution)/shard_map/all_to_all | solution.py:179
  72.5 315.1 %all-reduce.3.cloned.1.call-start = ((), (), s32[]{:S(2)}) async-start(), calls=%async_computation.2 | async-start | bytes 3145728 | tf_op jit(solution)/shard_map/psum | solution.py:45
  95.1 7.0 %collective-permute-start.3 = (bf16[1,128,256]{2,1,0:T(8,128)(2,1)S(1)}, bf16[1,128,256]{2,1,0:T(8,128)(2,1)S(1)}, u32[]{:S(2)}, u32[]{:S(2)}) collective-permute-start(bf16[1,128,256]{2,1,0:T(8,128)(2,1)S(1)} %bitcast.126), channel_id=1, source_target_pairs={{8,0},{16,8},{24,16},{32,24},{40,32},{48,40},{56,48},{64,56},{72,6... | collective-permute-start | bytes 196616 | tf_op jit(solution)/shard_map/ppermute | solution.py:23
  97.2 6.1 %collective-permute-start.2 = (bf16[1,128,256]{2,1,0:T(8,128)(2,1)S(1)}, bf16[1,128,256]{2,1,0:T(8,128)(2,1)S(1)}, u32[]{:S(2)}, u32[]{:S(2)}) collective-permute-start(bf16[1,128,256]{2,1,0:T(8,128)(2,1)S(1)} %bitcast.125), channel_id=1, source_target_pairs={{0,8},{8,16},{16,24},{24,32},{32,40},{40,48},{48,56},{56,64},{64,7... | collective-permute-start | bytes 196616 | tf_op jit(solution)/shard_map/ppermute | solution.py:21
  387.6 2.7 copy-start.6
  387.6 3.4 copy-start.2
Sparse Core Ops, SparseCore 0:
  104.7 282.8 all-reduce.2
where the time goes:
time: 400 us; the launch traced here: 399 us
  waiting for transfers between devices  296 us (74%)
  other arithmetic  28.7 us (7%)
  starting transfers between devices  28.3 us (7%)
  matrix products  16.7 us (4%)
  local copies, waits for them, and re-layouts  14.9 us (4%)
  between operations  14.4 us (4%)
    psum x1, waiting for transfers between devices, in_one(): subtotal = lax.psum(line, axis)  282 us
    scatter-add x1, other arithmetic, per_block(): totals.at[neighbour_index.reshape(-1)]  12.1 us
    all_to_all x1, starting transfers between devices, in_one_piece(): lax.all_to_all(both, axis, split_axis=split_dim, concat_axis=concat_dim,...  11.6 us
    all_to_all x1, waiting for transfers between devices, in_one_piece(): lax.all_to_all(both, axis, split_axis=split_dim, concat_axis=concat_dim,...  8.09 us
    ppermute x2, starting transfers between devices, with_halo(): lax.ppermute(tail, axis, [(i, (i + 1) % count) for i in range(ends)])  8.09 us
  transfers between devices with their start and end apart: 7, of which 4 were waited for; matrix products, arithmetic and copies ran while one was open for 2% of the time, Pallas kernels for 0%

commit v1 on v0

v1 whole, which is shorter than its diff:
```python
import math

import jax
import jax.numpy as jnp
import numpy as np
from jax import lax
from jax.experimental import pallas as pl
from jax.experimental.pallas import tpu as pltpu
from jax.sharding import Mesh
from jax.sharding import PartitionSpec as P

HEAD_DIM = 32
SNAPS = 8
HALO = 128
WIDTH = 256
SLOTS = 16
LANES = 128

FINE = (2, 4, 8, 4, 2)
FINE_NAMES = ("zl", "x", "y", "zh", "c")
DOM = ("zl", "x", "y")
SNAP = ("zh", "c")
SCATTER = ("zl", "y")
ACROSS = ("x", "zh")

f32 = jnp.float32
bf16 = jnp.bfloat16
VMEM = pl.BlockSpec(memory_space=pltpu.VMEM)


def call(kernel, outs, args, scratch=(), name=None):
    return pl.pallas_call(
        kernel,
        out_shape=[jax.ShapeDtypeStruct(s, d) for s, d in outs],
        in_specs=[VMEM] * len(args),
        out_specs=[VMEM] * len(outs),
        scratch_shapes=list(scratch),
        name=name,
    )(*args)


def mm(a, b):
    return jnp.dot(a, b, preferred_element_type=f32)


def mm_nt(a, b):
    return lax.dot_general(a, b, (((1,), (1,)), ((), ())), preferred_element_type=f32)


def mm_tn(a, b):
    return lax.dot_general(a, b, (((0,), (0,)), ((), ())), preferred_element_type=f32)


def put_slab(ref, index, value):
    base = index * 2 * WIDTH
    value = value.astype(ref.dtype)
    ref[base : base + WIDTH, :] = value[:, :LANES]
    ref[base + WIDTH : base + 2 * WIDTH, :] = value[:, LANES:]


def forward_kernel(left, own, right, nbr, deg, mproj, cproj, combined, spatial, slopew, ext, hot):
    ext[:HALO] = left[...]
    ext[HALO : HALO + 128] = own[...]
    ext[HALO + 128 :] = right[...]
    rows = own.shape[0]
    own_f = own[...].astype(f32)
    lanes = lax.broadcasted_iota(jnp.int32, (rows, 3 * HALO), 1)
    for k in range(SLOTS):
        mark = nbr[:, k : k + 1] == lanes
        hot[k * rows : (k + 1) * rows] = jnp.where(mark, 1.0, 0.0).astype(bf16)
    degree = deg[...]
    share = 1.0 / degree.astype(f32)
    total = jnp.zeros((rows, WIDTH), f32)
    group = 4
    for g in range(SLOTS // group):
        span = group * rows
        picked = mm(hot[g * span : (g + 1) * span], ext[...]).astype(bf16)
        message = mm(picked, mproj[...])
        for j in range(group):
            k = g * group + j
            weight = jnp.where(degree > k, share, 0.0)
            before = message[j * rows : (j + 1) * rows] + own_f
            logistic = 0.5 * jnp.tanh(0.5 * before) + 0.5
            value = before * logistic
            total = total + value * weight
            slope = logistic + logistic * (before - value)
            slopew[k * rows : (k + 1) * rows] = (slope * weight).astype(bf16)
    comb = total.astype(bf16)
    combined[...] = comb
    spatial[...] = (own_f + mm(comb, cproj[...])).astype(bf16)


def temporal_kernel(spat, cot, aproj, oproj, grad_spatial, attend_out, output_out, prods, sums):
    snaps, nodes, _ = spat.shape
    rows = snaps * nodes
    x = spat[...].reshape(rows, WIDTH)
    c = cot[...].reshape(rows, WIDTH)
    projected = mm(x, aproj[...])
    inverse_root = 1.0 / math.sqrt(HEAD_DIM)
    qs = projected[:, :WIDTH] * inverse_root
    key = projected[:, WIDTH : 2 * WIDTH]
    val = projected[:, 2 * WIDTH :]
    da = mm_nt(c, oproj[...])

    def split(at, value):
        high = value.astype(bf16)
        prods[at : at + rows, :WIDTH] = high
        prods[at : at + rows, WIDTH:] = (value - high.astype(f32)).astype(bf16)

    key3 = key.reshape(snaps, nodes, WIDTH)
    val3 = val.reshape(snaps, nodes, WIDTH)
    for s in range(snaps):
        one = slice(s * nodes, (s + 1) * nodes)
        split(s * rows, (qs[one][None] * key3).reshape(rows, WIDTH))
        split((snaps + s) * rows, (da[one][None] * val3).reshape(rows, WIDTH))
    i = lax.broadcasted_iota(jnp.int32, (2 * WIDTH, WIDTH), 0)
    j = lax.broadcasted_iota(jnp.int32, (2 * WIDTH, WIDTH), 1)
    same = (i & (WIDTH - 1)) // HEAD_DIM == j // HEAD_DIM
    same = jnp.where(same, 1.0, 0.0).astype(bf16)
    step = 4 * rows
    for at in range(0, 2 * snaps * rows, step):
        sums[at : at + step] = mm(prods[at : at + step], same)

    grad_key = jnp.zeros((snaps, nodes, WIDTH), f32)
    grad_val = jnp.zeros((snaps, nodes, WIDTH), f32)
    attended = []
    grad_query = []
    for s in range(snaps):
        one = slice(s * nodes, (s + 1) * nodes)
        exponent = jnp.exp(sums[s * rows : (s + 1) * rows]).reshape(snaps, nodes, WIDTH)
        soft = exponent * (1.0 / jnp.sum(exponent, axis=0))[None]
        attended.append(jnp.sum(soft * val3, axis=0))
        grad_soft = sums[(snaps + s) * rows : (snaps + s + 1) * rows].reshape(snaps, nodes, WIDTH)
        mean = jnp.sum(soft * grad_soft, axis=0)
        grad_score = soft * (grad_soft - mean[None])
        grad_query.append(jnp.sum(grad_score * key3, axis=0) * inverse_root)
        grad_key = grad_key + grad_score * qs[one][None]
        grad_val = grad_val + soft * da[one][None]
    att = jnp.concatenate(attended, axis=0).astype(bf16)
    put_slab(output_out, 0, mm_tn(att, c))
    parts = (
        jnp.concatenate(grad_query, axis=0).astype(bf16),
        grad_key.reshape(rows, WIDTH).astype(bf16),
        grad_val.reshape(rows, WIDTH).astype(bf16),
    )
    total = c.astype(f32)
    for p, part in enumerate(parts):
        put_slab(attend_out, p, mm_tn(x, part))
        total = total + mm_nt(part, aproj[:, p * WIDTH : (p + 1) * WIDTH])
    grad_spatial[...] = total.astype(bf16).reshape(snaps, nodes, WIDTH)


def backward_kernel(
    gs_ref, comb, slopew, nbrt, left, own, right, cproj, att_in, out_in,
    ghosts, own_rows, base, partial, hot, gb
):
    rows = own.shape[0]
    gs = gs_ref[...]
    gc = mm_nt(gs, cproj[...])
    below = lax.broadcasted_iota(jnp.int32, (3 * HALO, rows), 0)
    total = gs.astype(f32)
    for k in range(SLOTS):
        span = slice(k * rows, (k + 1) * rows)
        hot[:, span] = jnp.where(nbrt[k : k + 1, :] == below, 1.0, 0.0).astype(bf16)
        grad_before = gc * slopew[span].astype(f32)
        total = total + grad_before
        gb[span] = grad_before.astype(bf16)
    base[...] = total
    grad_rows = mm(hot[...], gb[...])
    ghosts[0] = grad_rows[:HALO].astype(bf16)
    ghosts[1] = grad_rows[HALO + rows :].astype(bf16)
    own_rows[...] = grad_rows[HALO : HALO + rows]
    rounded = grad_rows.astype(bf16)
    message = mm_tn(left[...], rounded[:HALO])
    message = message + mm_tn(own[...], rounded[HALO : HALO + rows])
    message = message + mm_tn(right[...], rounded[HALO + rows :])
    partial[0] = att_in[...]
    partial[1, : 2 * WIDTH] = out_in[...]
    second = partial.at[1]
    put_slab(second, 1, message)
    put_slab(second, 2, mm_tn(comb[...], gs))


def features_kernel(base, own_rows, from_left, from_right, mproj, grad):
    own = own_rows[...] + from_left[...].astype(f32) + from_right[...].astype(f32)
    grad[...] = (base[...] + mm_nt(own.astype(bf16), mproj[...])).astype(bf16)


def pair_kernel(both, out):
    out[...] = (both[0].astype(f32) + both[1].astype(f32)).astype(bf16).reshape(out.shape)


def fold_kernel(parts, out):
    total = parts[0].astype(f32)
    for p in range(1, parts.shape[0]):
        total = total + parts[p].astype(f32)
    total = total.astype(bf16)
    for p in range(out.shape[0]):
        out[p] = total


def final_kernel(factor, sums, message, combine, attend, output):
    def get(half, index):
        base = index * 2 * WIDTH
        first = sums[half, base : base + WIDTH, :].astype(f32) * factor
        second = sums[half, base + WIDTH : base + 2 * WIDTH, :].astype(f32) * factor
        return first, second

    def put(ref, at, pair):
        ref[:, at : at + LANES] = pair[0]
        ref[:, at + LANES : at + 2 * LANES] = pair[1]

    for p in range(3):
        put(attend, p * WIDTH, get(0, p))
    put(output, 0, get(1, 0))
    put(message, 0, get(1, 1))
    put(combine, 0, get(1, 2))


def swap(x, axes):
    return lax.all_to_all(x, axes, split_axis=0, concat_axis=0, tiled=True)


def body(features, cotangent, neighbours, degrees, mproj, cproj, aproj, oproj):
    _, rows, width = features.shape
    dom_size = lax.axis_size(DOM)
    up = [(i, i + 1) for i in range(dom_size - 1)]
    down = [(i + 1, i) for i in range(dom_size - 1)]
    own = features[0]
    from_left = lax.ppermute(own, DOM, up)
    from_right = lax.ppermute(own, DOM, down)
    first_row = lax.axis_index(DOM) * rows - HALO
    nbr = neighbours - first_row
    nbrt = nbr.T
    deg = degrees.reshape(rows, 1)
    edges = SLOTS * rows
    combined, spatial, slopew = call(
        forward_kernel,
        [((rows, width), bf16), ((rows, width), bf16), ((edges, width), bf16)],
        (from_left, own, from_right, nbr, deg, mproj, cproj),
        [pltpu.VMEM((3 * HALO, width), bf16), pltpu.VMEM((edges, 3 * HALO), bf16)],
        "forward",
    )
    share = rows // SNAPS
    sent = jnp.stack([spatial.reshape(SNAPS, share, width), cotangent[0].reshape(SNAPS, share, width)], axis=1)
    got = swap(sent, SNAP)
    grads, attend_part, output_part = call(
        temporal_kernel,
        [((SNAPS, share, width), bf16), ((6 * width, LANES), bf16), ((2 * width, LANES), bf16)],
        (got[:, 0], got[:, 1], aproj, oproj),
        [pltpu.VMEM((2 * SNAPS * rows, 2 * width), bf16), pltpu.VMEM((2 * SNAPS * rows, width), f32)],
        "temporal",
    )
    grad_spatial = swap(grads, SNAP).reshape(rows, width)
    ghosts, own_rows, base, partial = call(
        backward_kernel,
        [((2, HALO, width), bf16), ((rows, width), f32), ((rows, width), f32), ((2, 6 * width, LANES), bf16)],
        (grad_spatial, combined, slopew, nbrt, from_left, own, from_right, cproj, attend_part, output_part),
        [pltpu.VMEM((3 * HALO, edges), bf16), pltpu.VMEM((edges, width), bf16)],
        "backward",
    )
    back_left = lax.ppermute(ghosts[1], DOM, up)
    back_right = lax.ppermute(ghosts[0], DOM, down)
    (grad_features,) = call(
        features_kernel,
        [((rows, width), bf16)],
        (base, own_rows, back_left, back_right, mproj),
        name="features",
    )
    both = swap(partial, "c")
    count = lax.axis_size(SCATTER)
    across = lax.axis_size(ACROSS)
    piece = 6 * width // count
    (mine,) = call(pair_kernel, [((count, piece, LANES), bf16)], (both,), name="pair")
    (spread,) = call(fold_kernel, [((across, piece, LANES), bf16)], (swap(mine, SCATTER),), name="fold")
    (whole,) = call(fold_kernel, [((count, piece, LANES), bf16)], (swap(spread, ACROSS),), name="fold_all")
    half = swap(whole, SCATTER).reshape(6 * width, LANES)
    sums = lax.all_gather(half, "c", axis=0)
    factor = 1.0 / math.sqrt(SNAPS * dom_size * rows)

    def last(*refs):
        final_kernel(factor, *refs)

    message, combine, attend, output = call(
        last,
        [((width, width), f32), ((width, width), f32), ((width, 3 * width), f32), ((width, width), f32)],
        (sums,),
        name="final",
    )
    return grad_features[None], message, combine, attend, output


def build(mesh, fine):
    fine_mesh = Mesh(np.asarray(mesh.devices).reshape(fine), FINE_NAMES)
    in_specs = (
        P(SNAP, DOM, None),
        P(SNAP, DOM, None),
        P(DOM, None),
        P(DOM),
        P(),
        P(),
        P(),
        P(),
    )
    out_specs = (P(SNAP, DOM, None), P(), P(), P(), P())
    return jax.shard_map(body, mesh=fine_mesh, in_specs=in_specs, out_specs=out_specs, check_vma=False)


def solution(mesh):
    return build(mesh, FINE)
```

time: 400 us -> 141 us (0.35)
  the two profiles are of different devices: /device:TPU:17 before, /device:TPU:65 now
where the time goes in v1:
time: 141 us; the launch traced here: 140 us
  blocking collectives  61.1 us (43%)
  starting transfers between devices  30.5 us (22%)
  Pallas kernels  21.4 us (15%)
  waiting for transfers between devices  19 us (13%)
  local copies, waits for them, and re-layouts  5.38 us (4%)
  other arithmetic  1.45 us (1%)
    all_to_all x4, blocking collectives, swap(): return lax.all_to_all(x, axes, split_axis=0, concat_axis=0, tiled=True)  56.5 us
    pallas_call x8, Pallas kernels, call(): pl.pallas_call(kernel, out_shape=[jax.ShapeDtypeStruct(s, d) for s, d in...  21.4 us
    all_to_all x2, starting transfers between devices, swap(): return lax.all_to_all(x, axes, split_axis=0, concat_axis=0, tiled=True)  15.8 us
    all_to_all x2, waiting for transfers between devices, swap(): return lax.all_to_all(x, axes, split_axis=0, concat_axis=0, tiled=True)  6.88 us
    ppermute x1, starting transfers between devices, body(): from_right = lax.ppermute(own, DOM, down)  6.38 us
    ppermute x1, waiting for transfers between devices, body(): from_left = lax.ppermute(own, DOM, up)  4.67 us
    all_gather x1, blocking collectives, body(): sums = lax.all_gather(half, 'c', axis=0)  4.63 us
    ppermute x1, starting transfers between devices, body(): back_right = lax.ppermute(ghosts[0], DOM, down)  4.57 us
  transfers between devices with their start and end apart: 6, of which 4 were waited for; matrix products, arithmetic and copies ran while one was open for 1% of the time, Pallas kernels for 1%

profile of v1, /device:TPU:65, one launch (start us, length us, event | category | flops | bytes accessed | tf_op | source)
XLA Modules:
  0.0 139.7 jit_solution(18422279617509517832)
XLA Ops:
  0.6 6.4 %collective-permute-start.1 = (bf16[128,256]{1,0:T(8,128)(2,1)}, bf16[128,256]{1,0:T(8,128)(2,1)S(1)}, u32[]{:S(2)}, u32[]{:S(2)}) collective-permute-start(bf16[128,256]{1,0:T(8,128)(2,1)} %bitcast.24), channel_id=1, source_target_pairs={{8,0},{16,8},{24,16},{32,24},{40,32},{48,40},{56,48},{64,56},{72,6... | collective-permute-start | bytes 196616 | tf_op jit(solution)/shard_map/ppermute | solution.py:231
  7.0 1.9 %collective-permute-start = (bf16[128,256]{1,0:T(8,128)(2,1)}, bf16[128,256]{1,0:T(8,128)(2,1)S(1)}, u32[]{:S(2)}, u32[]{:S(2)}) collective-permute-start(bf16[128,256]{1,0:T(8,128)(2,1)} %bitcast.25), channel_id=1, source_target_pairs={{0,8},{8,16},{16,24},{24,32},{32,40},{40,48},{48,56},{56,64},{64,7... | collective-permute-start | bytes 196616 | tf_op jit(solution)/shard_map/ppermute | solution.py:230
  9.0 0.7 copy-done.7
  9.7 0.7 copy.15.nbr
  10.4 0.7 copy-done.8
  11.0 0.7 copy.16.deg
  11.8 4.7 %collective-permute-done.left = bf16[128,256]{1,0:T(8,128)(2,1)S(1)} collective-permute-done((bf16[128,256]{1,0:T(8,128)(2,1)}, bf16[128,256]{1,0:T(8,128)(2,1)S(1)}, u32[]{:S(2)}, u32[]{:S(2)}) %collective-permute-start) | collective-permute-done | bytes 65568 | tf_op jit(solution)/shard_map/ppermute | solution.py:230
  16.5 0.6 copy-done.1
  17.1 4.2 %forward.1 = (bf16[128,256]{1,0:T(8,128)(2,1)}, bf16[128,256]{1,0:T(8,128)(2,1)}, bf16[2048,256]{1,0:T(8,128)(2,1)}) custom-call(bf16[128,256]{1,0:T(8,128)(2,1)} %copy-done.1, bf16[128,256]{1,0:T(8,128)(2,1)} %bitcast.26, bf16[128,256]{1,0:T(8,128)(2,1)} %copy-done, s32[128,16]{1,0:T(8,128)} %copy.15.nbr, s32[128,1]{1,0:T(8,128)} %copy.16.deg, ...), custom_call_target="tpu_custom_call" | custom-call | tf_op jit(solution)/shard_map/forward/pallas_call | solution.py:32
  21.3 0.9 pad_maximum_fusion
  22.2 20.2 %all_to_all.30 = bf16[8,2,16,256]{3,2,1,0:T(8,128)(2,1)S(1)} all-to-all(bf16[8,2,16,256]{3,2,1,0:T(8,128)(2,1)S(1)} %pad_maximum_fusion), channel_id=1, replica_groups=mesh['zl'=2,'x'=4,'y'=8,'zh'=4,'c'=2] {'zh','c'}, dimensions={0} | all-to-all | bytes 262144 | tf_op jit(solution)/shard_map/all_to_all | solution.py:221
  42.4 0.7 slice_bitcast_fusion
  43.0 3.4 %temporal.1 = (bf16[8,16,256]{2,1,0:T(8,128)(2,1)}, bf16[1536,128]{1,0:T(8,128)(2,1)}, bf16[512,128]{1,0:T(8,128)(2,1)}) custom-call(bf16[8,16,256]{2,1,0:T(8,128)(2,1)} %get-tuple-element.36.spat, bf16[8,16,256]{2,1,0:T(8,128)(2,1)} %get-tuple-element.35.cot, bf16[256,768]{1,0:T(8,128)(2,1)} %aproj.1, bf16[256,256]{1,0:T(8,128)(2,1)} %oproj.1), custom_call_target="tpu_custom_call" | custom-call | tf_op jit(solution)/shard_map/temporal/pallas_call | solution.py:32
  46.4 4.5 %all-to-all-start.1 = ((bf16[8,16,256]{2,1,0:T(8,128)(2,1)}), bf16[8,16,256]{2,1,0:T(8,128)(2,1)S(1)}, u32[]{:S(2)}, u32[]{:S(2)}) async-start(bf16[8,16,256]{2,1,0:T(8,128)(2,1)} %get-tuple-element.20), calls=%async_computation.1 | async-start | bytes 131072 | tf_op jit(solution)/shard_map/all_to_all | solution.py:221
  51.5 6.9 %all-to-all-done.1 = bf16[8,16,256]{2,1,0:T(8,128)(2,1)S(1)} async-done(((bf16[8,16,256]{2,1,0:T(8,128)(2,1)}), bf16[8,16,256]{2,1,0:T(8,128)(2,1)S(1)}, u32[]{:S(2)}, u32[]{:S(2)}) %all-to-all-start.1) | async-done | bytes 65568 | tf_op jit(solution)/shard_map/all_to_all | solution.py:221
  58.4 0.6 copy-done.2
  59.0 4.0 %backward.1 = (bf16[2,128,256]{2,1,0:T(8,128)(2,1)}, f32[128,256]{1,0:T(8,128)}, f32[128,256]{1,0:T(8,128)}, bf16[2,1536,128]{2,1,0:T(8,128)(2,1)}) custom-call(bf16[128,256]{1,0:T(8,128)(2,1)} %bitcast.28, bf16[128,256]{1,0:T(8,128)(2,1)} %get-tuple-element.21.comb, bf16[2048,256]{1,0:T(8,128)(2,1)} %get-tuple-element.22.slopew, s32[16,128]{1,0:T(8,128)} %fusion.nbrt, ...), custom_call_target="tpu_custom_call" | custom-call | tf_op jit(solution)/shard_map/backward/pallas_call | solution.py:32
  63.0 6.8 %all_to_all.31.both = bf16[2,1536,128]{2,1,0:T(8,128)(2,1)} all-to-all(bf16[2,1536,128]{2,1,0:T(8,128)(2,1)} %get-tuple-element.28), channel_id=1, replica_groups=mesh['zl'=2,'x'=4,'y'=8,'zh'=4,'c'=2] {'c'}, dimensions={0} | all-to-all | bytes 1572864 | tf_op jit(solution)/shard_map/all_to_all | solution.py:221
  69.8 2.0 %pair.1 = bf16[16,96,128]{2,1,0:T(8,128)(2,1)} custom-call(bf16[2,1536,128]{2,1,0:T(8,128)(2,1)} %all_to_all.31.both), custom_call_target="tpu_custom_call" | custom-call | tf_op jit(solution)/shard_map/pair/pallas_call | solution.py:32
  71.7 12.9 %all_to_all.32.parts = bf16[16,96,128]{2,1,0:T(8,128)(2,1)} all-to-all(bf16[16,96,128]{2,1,0:T(8,128)(2,1)} %pair.1), channel_id=1, replica_groups=mesh['zl'=2,'x'=4,'y'=8,'zh'=4,'c'=2] {'zl','y'}, dimensions={0} | all-to-all | bytes 786432 | tf_op jit(solution)/shard_map/all_to_all | solution.py:221
  84.7 1.8 %fold.1 = bf16[16,96,128]{2,1,0:T(8,128)(2,1)} custom-call(bf16[16,96,128]{2,1,0:T(8,128)(2,1)} %all_to_all.32.parts), custom_call_target="tpu_custom_call" | custom-call | tf_op jit(solution)/shard_map/fold/pallas_call | solution.py:32
  86.5 16.6 %all_to_all.33.parts = bf16[16,96,128]{2,1,0:T(8,128)(2,1)} all-to-all(bf16[16,96,128]{2,1,0:T(8,128)(2,1)} %fold.1), channel_id=1, replica_groups=mesh['zl'=2,'x'=4,'y'=8,'zh'=4,'c'=2] {'x','zh'}, dimensions={0} | all-to-all | bytes 786432 | tf_op jit(solution)/shard_map/all_to_all | solution.py:221
  103.1 1.8 %fold_all.1 = bf16[16,96,128]{2,1,0:T(8,128)(2,1)} custom-call(bf16[16,96,128]{2,1,0:T(8,128)(2,1)} %all_to_all.33.parts), custom_call_target="tpu_custom_call" | custom-call | tf_op jit(solution)/shard_map/fold_all/pallas_call | solution.py:32
  104.9 11.3 %all-to-all-start.5 = ((bf16[16,96,128]{2,1,0:T(8,128)(2,1)}), bf16[16,96,128]{2,1,0:T(8,128)(2,1)S(1)}, u32[]{:S(2)}, u32[]{:S(2)}) async-start(bf16[16,96,128]{2,1,0:T(8,128)(2,1)} %fold_all.1), calls=%async_computation.5 | async-start | bytes 786432 | tf_op jit(solution)/shard_map/all_to_all | solution.py:221
  116.2 4.6 %collective-permute-start.3 = (bf16[128,256]{1,0:T(8,128)(2,1)S(1)}, bf16[128,256]{1,0:T(8,128)(2,1)S(1)}, u32[]{:S(2)}, u32[]{:S(2)}) collective-permute-start(bf16[128,256]{1,0:T(8,128)(2,1)S(1)} %get-tuple-element.33), channel_id=1, source_target_pairs={{8,0},{16,8},{24,16},{32,24},{40,32},{48,40},{56,48},{64,56},{72,6... | collective-permute-start | bytes 196616 | tf_op jit(solution)/shard_map/ppermute | solution.py:263
  120.8 1.9 %collective-permute-start.2 = (bf16[128,256]{1,0:T(8,128)(2,1)S(1)}, bf16[128,256]{1,0:T(8,128)(2,1)S(1)}, u32[]{:S(2)}, u32[]{:S(2)}) collective-permute-start(bf16[128,256]{1,0:T(8,128)(2,1)S(1)} %get-tuple-element.34), channel_id=1, source_target_pairs={{0,8},{8,16},{16,24},{24,32},{32,40},{40,48},{48,56},{56,64},{64,7... | collective-permute-start | bytes 196616 | tf_op jit(solution)/shard_map/ppermute | solution.py:262
  122.7 4.5 %collective-permute-done.3.from_right = bf16[128,256]{1,0:T(8,128)(2,1)S(1)} collective-permute-done((bf16[128,256]{1,0:T(8,128)(2,1)S(1)}, bf16[128,256]{1,0:T(8,128)(2,1)S(1)}, u32[]{:S(2)}, u32[]{:S(2)}) %collective-permute-start.3) | collective-permute-done | bytes 65568 | tf_op jit(solution)/shard_map/ppermute | solution.py:263
  127.2 3.0 %collective-permute-done.2.from_left = bf16[128,256]{1,0:T(8,128)(2,1)S(1)} collective-permute-done((bf16[128,256]{1,0:T(8,128)(2,1)S(1)}, bf16[128,256]{1,0:T(8,128)(2,1)S(1)}, u32[]{:S(2)}, u32[]{:S(2)}) %collective-permute-start.2) | collective-permute-done | bytes 65568 | tf_op jit(solution)/shard_map/ppermute | solution.py:262
  130.2 0.6 copy-done.5
  130.8 1.9 %features.1 = bf16[128,256]{1,0:T(8,128)(2,1)} custom-call(f32[128,256]{1,0:T(8,128)} %get-tuple-element.25.base, f32[128,256]{1,0:T(8,128)} %get-tuple-element.26.own_rows, bf16[128,256]{1,0:T(8,128)(2,1)} %copy-done.5, bf16[128,256]{1,0:T(8,128)(2,1)} %copy-done.4, bf16[256,256]{1,0:T(8,128)(2,1)} %mproj.3), custom_call_target="tpu_custom_call" | custom-call | tf_op jit(solution)/shard_map/features/pallas_call | solution.py:32
  132.7 4.6 %all_gather.3.refs_0_ = bf16[2,1536,128]{2,1,0:T(8,128)(2,1)} all-gather(bf16[1,1536,128]{2,1,0:T(8,128)(2,1)S(1)} %bitcast.23), channel_id=1, replica_groups=mesh['zl'=2,'x'=4,'y'=8,'zh'=4,'c'=2] {'c'}, dimensions={0}, use_global_device_ids=true | all-gather | bytes 1179648 | tf_op jit(solution)/shard_map/all_gather | solution.py:278
  137.4 2.3 %final.1 = (f32[256,256]{1,0:T(8,128)}, f32[256,256]{1,0:T(8,128)}, f32[256,768]{1,0:T(8,128)}, f32[256,256]{1,0:T(8,128)}) custom-call(bf16[2,1536,128]{2,1,0:T(8,128)(2,1)} %all_gather.3.refs_0_), custom_call_target="tpu_custom_call" | custom-call | tf_op jit(solution)/shard_map/final/pallas_call | solution.py:32
  (18 shorter events, 0.6 us)
Async XLA Ops:
  0.6 11.2 %collective-permute-start.1 = (bf16[128,256]{1,0:T(8,128)(2,1)}, bf16[128,256]{1,0:T(8,128)(2,1)S(1)}, u32[]{:S(2)}, u32[]{:S(2)}) collective-permute-start(bf16[128,256]{1,0:T(8,128)(2,1)} %bitcast.24), channel_id=1, source_target_pairs={{8,0},{16,8},{24,16},{32,24},{40,32},{48,40},{56,48},{64,56},{72,6... | collective-permute-start | bytes 196616 | tf_op jit(solution)/shard_map/ppermute | solution.py:231
  7.0 9.4 %collective-permute-start = (bf16[128,256]{1,0:T(8,128)(2,1)}, bf16[128,256]{1,0:T(8,128)(2,1)S(1)}, u32[]{:S(2)}, u32[]{:S(2)}) collective-permute-start(bf16[128,256]{1,0:T(8,128)(2,1)} %bitcast.25), channel_id=1, source_target_pairs={{0,8},{8,16},{16,24},{24,32},{32,40},{40,48},{48,56},{56,64},{64,7... | collective-permute-start | bytes 196616 | tf_op jit(solution)/shard_map/ppermute | solution.py:230
  9.0 0.7 copy-start.7
  10.4 0.7 copy-start.8
  11.8 9.5 %copy-start.6 = (bf16[1,128,256]{2,1,0:T(8,128)(2,1)S(1)}, bf16[1,128,256]{2,1,0:T(8,128)(2,1)}, u32[]{:S(2)}) copy-start(bf16[1,128,256]{2,1,0:T(8,128)(2,1)} %param.9) | copy-start | bytes 196612
  11.8 4.7 %copy-start = (bf16[128,256]{1,0:T(8,128)(2,1)}, bf16[128,256]{1,0:T(8,128)(2,1)S(1)}, u32[]{:S(2)}) copy-start(bf16[128,256]{1,0:T(8,128)(2,1)S(1)} %collective-permute-done.1.right) | copy-start | bytes 196612
  16.5 0.6 copy-start.1
  46.4 11.9 %all-to-all-start.1 = ((bf16[8,16,256]{2,1,0:T(8,128)(2,1)}), bf16[8,16,256]{2,1,0:T(8,128)(2,1)S(1)}, u32[]{:S(2)}, u32[]{:S(2)}) async-start(bf16[8,16,256]{2,1,0:T(8,128)(2,1)} %get-tuple-element.20), calls=%async_computation.1 | async-start | bytes 131072 | tf_op jit(solution)/shard_map/all_to_all | solution.py:221
  58.4 0.6 copy-start.2
  104.9 11.3 %copy-start.3 = (bf16[2,128,256]{2,1,0:T(8,128)(2,1)S(1)}, bf16[2,128,256]{2,1,0:T(8,128)(2,1)}, u32[]{:S(2)}) copy-start(bf16[2,128,256]{2,1,0:T(8,128)(2,1)} %get-tuple-element.27) | copy-start | bytes 393220
  104.9 27.8 %all-to-all-start.5 = ((bf16[16,96,128]{2,1,0:T(8,128)(2,1)}), bf16[16,96,128]{2,1,0:T(8,128)(2,1)S(1)}, u32[]{:S(2)}, u32[]{:S(2)}) async-start(bf16[16,96,128]{2,1,0:T(8,128)(2,1)} %fold_all.1), calls=%async_computation.5 | async-start | bytes 786432 | tf_op jit(solution)/shard_map/all_to_all | solution.py:221
  116.2 11.0 %collective-permute-start.3 = (bf16[128,256]{1,0:T(8,128)(2,1)S(1)}, bf16[128,256]{1,0:T(8,128)(2,1)S(1)}, u32[]{:S(2)}, u32[]{:S(2)}) collective-permute-start(bf16[128,256]{1,0:T(8,128)(2,1)S(1)} %get-tuple-element.33), channel_id=1, source_target_pairs={{8,0},{16,8},{24,16},{32,24},{40,32},{48,40},{56,48},{64,56},{72,6... | collective-permute-start | bytes 196616 | tf_op jit(solution)/shard_map/ppermute | solution.py:263
  120.8 9.4 %collective-permute-start.2 = (bf16[128,256]{1,0:T(8,128)(2,1)S(1)}, bf16[128,256]{1,0:T(8,128)(2,1)S(1)}, u32[]{:S(2)}, u32[]{:S(2)}) collective-permute-start(bf16[128,256]{1,0:T(8,128)(2,1)S(1)} %get-tuple-element.34), channel_id=1, source_target_pairs={{0,8},{8,16},{16,24},{24,32},{32,40},{40,48},{48,56},{56,64},{64,7... | collective-permute-start | bytes 196616 | tf_op jit(solution)/shard_map/ppermute | solution.py:262
  127.2 3.0 %copy-start.4 = (bf16[128,256]{1,0:T(8,128)(2,1)}, bf16[128,256]{1,0:T(8,128)(2,1)S(1)}, u32[]{:S(2)}) copy-start(bf16[128,256]{1,0:T(8,128)(2,1)S(1)} %collective-permute-done.3.from_right) | copy-start | bytes 196612
  130.2 0.6 copy-start.5

commit v2 on v1

--- a/solution.py
+++ b/solution.py
@@ -9,6 +9,7 @@
 from jax.sharding import Mesh
 from jax.sharding import PartitionSpec as P
 
+
 HEAD_DIM = 32
 SNAPS = 8
 HALO = 128
@@ -26,17 +27,22 @@
 f32 = jnp.float32
 bf16 = jnp.bfloat16
 VMEM = pl.BlockSpec(memory_space=pltpu.VMEM)
-
-
-def call(kernel, outs, args, scratch=(), name=None):
+SMEM = pl.BlockSpec(memory_space=pltpu.SMEM)
+
+
+def call(kernel, outs, args, scratch=(), scalars=0, stored=False):
+    bound = []
+    for n, a in enumerate(args):
+        bound.append(a if n < scalars else pltpu.with_memory_space_constraint(a, pltpu.VMEM))
+    place = jax.ShapeDtypeStruct if stored else pltpu.VMEM
     return pl.pallas_call(
         kernel,
-        out_shape=[jax.ShapeDtypeStruct(s, d) for s, d in outs],
-        in_specs=[VMEM] * len(args),
+        out_shape=[place(s, d) for s, d in outs],
+        in_specs=[SMEM if n < scalars else VMEM for n in range(len(args))],
         out_specs=[VMEM] * len(outs),
         scratch_shapes=list(scratch),
-        name=name,
-    )(*args)
+        compiler_params=pltpu.CompilerParams(vmem_limit_bytes=24 * 2**20),
+    )(*bound)
 
 
 def mm(a, b):
@@ -58,18 +64,38 @@
     ref[base + WIDTH : base + 2 * WIDTH, :] = value[:, LANES:]
 
 
-def forward_kernel(left, own, right, nbr, deg, mproj, cproj, combined, spatial, slopew, ext, hot):
+def slots_kernel(
+    first_row, nbr_in, deg_in, own, cot, mproj, cproj,
+    hot, weights, nbrt, own_out, cot_out, mproj_out, cproj_out, table_in, deg, sems
+):
+    moves = ((nbr_in, table_in), (deg_in, deg), (own, own_out), (cot, cot_out), (mproj, mproj_out), (cproj, cproj_out))
+    copies = [pltpu.make_async_copy(a, b, sems.at[n]) for n, (a, b) in enumerate(moves)]
+    for copy in copies:
+        copy.start()
+    copies[0].wait()
+    copies[1].wait()
+    slots, rows = nbrt.shape
+    local = table_in[...] - first_row[0]
+    nbrt[...] = local
+    pad = jnp.zeros((rows - slots - 1, rows), f32)
+    table = jnp.concatenate([local.astype(f32), deg[...].astype(f32), pad], axis=0).T
+    lanes = lax.broadcasted_iota(jnp.int32, (rows, 3 * HALO), 1).astype(f32)
+    for k in range(slots):
+        mark = table[:, k : k + 1] == lanes
+        hot[k * rows : (k + 1) * rows] = jnp.where(mark, 1.0, 0.0).astype(bf16)
+    degree = table[:, slots : slots + 1]
+    slot = lax.broadcasted_iota(jnp.int32, (rows, slots), 1).astype(f32)
+    weights[...] = jnp.where(slot < degree, 1.0 / degree, 0.0)
+    for copy in copies[2:]:
+        copy.wait()
+
+
+def forward_kernel(left, own, right, cot, hot, weights, mproj, cproj, combined, sent, slopew, ext):
     ext[:HALO] = left[...]
     ext[HALO : HALO + 128] = own[...]
     ext[HALO + 128 :] = right[...]
     rows = own.shape[0]
     own_f = own[...].astype(f32)
-    lanes = lax.broadcasted_iota(jnp.int32, (rows, 3 * HALO), 1)
-    for k in range(SLOTS):
-        mark = nbr[:, k : k + 1] == lanes
-        hot[k * rows : (k + 1) * rows] = jnp.where(mark, 1.0, 0.0).astype(bf16)
-    degree = deg[...]
-    share = 1.0 / degree.astype(f32)
     total = jnp.zeros((rows, WIDTH), f32)
     group = 4
     for g in range(SLOTS // group):
@@ -78,7 +104,7 @@
         message = mm(picked, mproj[...])
         for j in range(group):
             k = g * group + j
-            weight = jnp.where(degree > k, share, 0.0)
+            weight = weights[:, k : k + 1]
             before = message[j * rows : (j + 1) * rows] + own_f
             logistic = 0.5 * jnp.tanh(0.5 * before) + 0.5
             value = before * logistic
@@ -87,14 +113,18 @@
             slopew[k * rows : (k + 1) * rows] = (slope * weight).astype(bf16)
     comb = total.astype(bf16)
     combined[...] = comb
-    spatial[...] = (own_f + mm(comb, cproj[...])).astype(bf16)
-
-
-def temporal_kernel(spat, cot, aproj, oproj, grad_spatial, attend_out, output_out, prods, sums):
-    snaps, nodes, _ = spat.shape
+    spatial = (own_f + mm(comb, cproj[...])).astype(bf16)
+    share = sent.shape[2]
+    for s in range(sent.shape[0]):
+        sent[s, 0] = spatial[s * share : (s + 1) * share]
+        sent[s, 1] = cot[s * share : (s + 1) * share]
+
+
+def temporal_kernel(got, aproj, oproj, grad_spatial, attend_out, output_out, prods, sums):
+    snaps, _, nodes, _ = got.shape
     rows = snaps * nodes
-    x = spat[...].reshape(rows, WIDTH)
-    c = cot[...].reshape(rows, WIDTH)
+    x = got[:, 0].reshape(rows, WIDTH)
+    c = got[:, 1].reshape(rows, WIDTH)
     projected = mm(x, aproj[...])
     inverse_root = 1.0 / math.sqrt(HEAD_DIM)
     qs = projected[:, :WIDTH] * inverse_root
@@ -151,14 +181,14 @@
 
 
 def backward_kernel(
-    gs_ref, comb, slopew, nbrt, left, own, right, cproj, att_in, out_in,
-    ghosts, own_rows, base, partial, hot, gb
+    core, gs_ref, comb, slopew, nbrt, left, own, right, cproj, att_in, out_in,
+    to_left, to_right, own_rows, base, keep, send, gb, other, hot
 ):
     rows = own.shape[0]
     gs = gs_ref[...]
     gc = mm_nt(gs, cproj[...])
+    total = gs.astype(f32)
     below = lax.broadcasted_iota(jnp.int32, (3 * HALO, rows), 0)
-    total = gs.astype(f32)
     for k in range(SLOTS):
         span = slice(k * rows, (k + 1) * rows)
         hot[:, span] = jnp.where(nbrt[k : k + 1, :] == below, 1.0, 0.0).astype(bf16)
@@ -167,18 +197,19 @@
         gb[span] = grad_before.astype(bf16)
     base[...] = total
     grad_rows = mm(hot[...], gb[...])
-    ghosts[0] = grad_rows[:HALO].astype(bf16)
-    ghosts[1] = grad_rows[HALO + rows :].astype(bf16)
+    rounded = grad_rows.astype(bf16)
+    to_left[...] = rounded[:HALO]
+    to_right[...] = rounded[HALO + rows :]
     own_rows[...] = grad_rows[HALO : HALO + rows]
-    rounded = grad_rows.astype(bf16)
     message = mm_tn(left[...], rounded[:HALO])
     message = message + mm_tn(own[...], rounded[HALO : HALO + rows])
     message = message + mm_tn(right[...], rounded[HALO + rows :])
-    partial[0] = att_in[...]
-    partial[1, : 2 * WIDTH] = out_in[...]
-    second = partial.at[1]
-    put_slab(second, 1, message)
-    put_slab(second, 2, mm_tn(comb[...], gs))
+    other[: 2 * WIDTH] = out_in[...]
+    put_slab(other, 1, message)
+    put_slab(other, 2, mm_tn(comb[...], gs))
+    first = core[0] == 0
+    keep[...] = jnp.where(first, att_in[...], other[...])
+    send[0] = jnp.where(first, other[...], att_in[...])
 
 
 def features_kernel(base, own_rows, from_left, from_right, mproj, grad):
@@ -186,8 +217,9 @@
     grad[...] = (base[...] + mm_nt(own.astype(bf16), mproj[...])).astype(bf16)
 
 
-def pair_kernel(both, out):
-    out[...] = (both[0].astype(f32) + both[1].astype(f32)).astype(bf16).reshape(out.shape)
+def pair_kernel(core, keep, both, out):
+    other = jnp.where(core[0] == 0, both[1], both[0])
+    out[...] = (keep[...].astype(f32) + other.astype(f32)).astype(bf16).reshape(out.shape)
 
 
 def fold_kernel(parts, out):
@@ -221,61 +253,87 @@
     return lax.all_to_all(x, axes, split_axis=0, concat_axis=0, tiled=True)
 
 
-def body(features, cotangent, neighbours, degrees, mproj, cproj, aproj, oproj):
+def step(features, cotangent, neighbours, degrees, mproj, cproj, aproj, oproj):
     _, rows, width = features.shape
     dom_size = lax.axis_size(DOM)
     up = [(i, i + 1) for i in range(dom_size - 1)]
     down = [(i + 1, i) for i in range(dom_size - 1)]
     own = features[0]
+    cot = cotangent[0]
     from_left = lax.ppermute(own, DOM, up)
     from_right = lax.ppermute(own, DOM, down)
-    first_row = lax.axis_index(DOM) * rows - HALO
-    nbr = neighbours - first_row
-    nbrt = nbr.T
-    deg = degrees.reshape(rows, 1)
+    first_row = (lax.axis_index(DOM) * rows - HALO).reshape(1)
+    core = lax.axis_index("c").reshape(1)
     edges = SLOTS * rows
-    combined, spatial, slopew = call(
+    stored = [
+        pltpu.with_memory_space_constraint(a, pltpu.HBM)
+        for a in (neighbours.T, degrees.reshape(1, rows), own, cot, mproj, cproj)
+    ]
+    hot, weights, nbrt, own, cot, mproj, cproj = pl.pallas_call(
+        slots_kernel,
+        out_shape=[
+            pltpu.VMEM((edges, 3 * HALO), bf16),
+            pltpu.VMEM((rows, SLOTS), f32),
+            pltpu.VMEM((SLOTS, rows), jnp.int32),
+            pltpu.VMEM((rows, width), bf16),
+            pltpu.VMEM((rows, width), bf16),
+            pltpu.VMEM((width, width), bf16),
+            pltpu.VMEM((width, width), bf16),
+        ],
+        in_specs=[SMEM] + [pl.BlockSpec(memory_space=pl.ANY)] * 6,
+        out_specs=[VMEM] * 7,
+        scratch_shapes=[
+            pltpu.VMEM((SLOTS, rows), jnp.int32),
+            pltpu.VMEM((1, rows), jnp.int32),
+            pltpu.SemaphoreType.DMA((6,)),
+        ],
+        compiler_params=pltpu.CompilerParams(vmem_limit_bytes=24 * 2**20),
+        name="slots",
+    )(first_row, *stored)
+    combined, sent, slopew = call(
         forward_kernel,
-        [((rows, width), bf16), ((rows, width), bf16), ((edges, width), bf16)],
-        (from_left, own, from_right, nbr, deg, mproj, cproj),
-        [pltpu.VMEM((3 * HALO, width), bf16), pltpu.VMEM((edges, 3 * HALO), bf16)],
-        "forward",
-    )
-    share = rows // SNAPS
-    sent = jnp.stack([spatial.reshape(SNAPS, share, width), cotangent[0].reshape(SNAPS, share, width)], axis=1)
+        [((rows, width), bf16), ((SNAPS, 2, rows // SNAPS, width), bf16), ((edges, width), bf16)],
+        (from_left, own, from_right, cot, hot, weights, mproj, cproj),
+        [pltpu.VMEM((3 * HALO, width), bf16)],
+    )
     got = swap(sent, SNAP)
     grads, attend_part, output_part = call(
         temporal_kernel,
-        [((SNAPS, share, width), bf16), ((6 * width, LANES), bf16), ((2 * width, LANES), bf16)],
-        (got[:, 0], got[:, 1], aproj, oproj),
+        [((SNAPS, rows // SNAPS, width), bf16), ((6 * width, LANES), bf16), ((2 * width, LANES), bf16)],
+        (got, aproj, oproj),
         [pltpu.VMEM((2 * SNAPS * rows, 2 * width), bf16), pltpu.VMEM((2 * SNAPS * rows, width), f32)],
-        "temporal",
     )
     grad_spatial = swap(grads, SNAP).reshape(rows, width)
-    ghosts, own_rows, base, partial = call(
+    to_left, to_right, own_rows, base, keep, send = call(
         backward_kernel,
-        [((2, HALO, width), bf16), ((rows, width), f32), ((rows, width), f32), ((2, 6 * width, LANES), bf16)],
-        (grad_spatial, combined, slopew, nbrt, from_left, own, from_right, cproj, attend_part, output_part),
-        [pltpu.VMEM((3 * HALO, edges), bf16), pltpu.VMEM((edges, width), bf16)],
-        "backward",
-    )
-    back_left = lax.ppermute(ghosts[1], DOM, up)
-    back_right = lax.ppermute(ghosts[0], DOM, down)
+        [
+            ((HALO, width), bf16),
+            ((HALO, width), bf16),
+            ((rows, width), f32),
+            ((rows, width), f32),
+            ((6 * width, LANES), bf16),
+            ((1, 6 * width, LANES), bf16),
+        ],
+        (core, grad_spatial, combined, slopew, nbrt, from_left, own, from_right, cproj, attend_part, output_part),
+        [pltpu.VMEM((edges, width), bf16), pltpu.VMEM((6 * width, LANES), bf16), pltpu.VMEM((3 * HALO, edges), bf16)],
+        scalars=1,
+    )
+    back_left = lax.ppermute(to_right, DOM, up)
+    back_right = lax.ppermute(to_left, DOM, down)
     (grad_features,) = call(
-        features_kernel,
-        [((rows, width), bf16)],
-        (base, own_rows, back_left, back_right, mproj),
-        name="features",
-    )
-    both = swap(partial, "c")
+        features_kernel, [((rows, width), bf16)], (base, own_rows, back_left, back_right, mproj), stored=True
+    )
+    both = lax.all_gather(send, "c", axis=0, tiled=True)
     count = lax.axis_size(SCATTER)
     across = lax.axis_size(ACROSS)
     piece = 6 * width // count
-    (mine,) = call(pair_kernel, [((count, piece, LANES), bf16)], (both,), name="pair")
-    (spread,) = call(fold_kernel, [((across, piece, LANES), bf16)], (swap(mine, SCATTER),), name="fold")
-    (whole,) = call(fold_kernel, [((count, piece, LANES), bf16)], (swap(spread, ACROSS),), name="fold_all")
-    half = swap(whole, SCATTER).reshape(6 * width, LANES)
-    sums = lax.all_gather(half, "c", axis=0)
+    (mine,) = call(pair_kernel, [((count, piece, LANES), bf16)], (core, keep, both), scalars=1)
+    parts = swap(mine, SCATTER)
+    (spread,) = call(fold_kernel, [((across, piece, LANES), bf16)], (parts,))
+    parts = swap(spread, ACROSS)
+    (whole,) = call(fold_kernel, [((count, piece, LANES), bf16)], (parts,))
+    half = swap(whole, SCATTER).reshape(1, 6 * width, LANES)
+    sums = lax.all_gather(half, "c", axis=0, tiled=True)
     factor = 1.0 / math.sqrt(SNAPS * dom_size * rows)
 
     def last(*refs):
@@ -285,7 +343,7 @@
         last,
         [((width, width), f32), ((width, width), f32), ((width, 3 * width), f32), ((width, width), f32)],
         (sums,),
-        name="final",
+        stored=True,
     )
     return grad_features[None], message, combine, attend, output
 
@@ -303,7 +361,7 @@
         P(),
     )
     out_specs = (P(SNAP, DOM, None), P(), P(), P(), P())
-    return jax.shard_map(body, mesh=fine_mesh, in_specs=in_specs, out_specs=out_specs, check_vma=False)
+    return jax.shard_map(step, mesh=fine_mesh, in_specs=in_specs, out_specs=out_specs, check_vma=False)
 
 
 def solution(mesh):

time: 141 us -> 116 us (0.82)
  the two profiles are of different devices: /device:TPU:65 before, /device:TPU:63 now
where the time goes in v2:
time: 116 us
  blocking collectives  62.6 us (54%)
  starting transfers between devices  27 us (23%)
  waiting for transfers between devices  15.3 us (13%)
  Pallas kernels  10 us (9%)
    all_to_all x3, blocking collectives, swap(): return lax.all_to_all(x, axes, split_axis=0, concat_axis=0, tiled=True)  54.1 us
    all_to_all x2, starting transfers between devices, swap(): return lax.all_to_all(x, axes, split_axis=0, concat_axis=0, tiled=True)  10.5 us
    pallas_call x8, Pallas kernels, call(): pl.pallas_call(kernel, out_shape=[place(s, d) for s, d in outs], in_specs...  8.72 us
    all_to_all x2, waiting for transfers between devices, swap(): return lax.all_to_all(x, axes, split_axis=0, concat_axis=0, tiled=True)  7.28 us
    ppermute x1, starting transfers between devices, step(): from_left = lax.ppermute(own, DOM, up)  6.52 us
    all_gather x1, blocking collectives, step(): sums = lax.all_gather(half, 'c', axis=0, tiled=True)  5.53 us
    ppermute x1, waiting for transfers between devices, step(): back_right = lax.ppermute(to_left, DOM, down)  5.33 us
    ppermute x1, starting transfers between devices, step(): back_left = lax.ppermute(to_right, DOM, up)  4.85 us
  transfers between devices with their start and end apart: 6, of which 4 were waited for; matrix products, arithmetic and copies ran while one was open for 0% of the time, Pallas kernels for 2%

profile of v2, /device:TPU:63, one launch (start us, length us, event | category | flops | bytes accessed | tf_op | source)
XLA Modules:
  0.0 115.6 jit_solution(16301517586281392496)
XLA Ops:
  0.6 0.0 copy-start.1
  0.6 0.0 copy-start
  0.7 3.1 %collective-permute-start.1 = (bf16[128,256]{1,0:T(8,128)(2,1)}, bf16[128,256]{1,0:T(8,128)(2,1)S(1)}, u32[]{:S(2)}, u32[]{:S(2)}) collective-permute-start(bf16[128,256]{1,0:T(8,128)(2,1)} %bitcast.12), channel_id=1, source_target_pairs={{8,0},{16,8},{24,16},{32,24},{40,32},{48,40},{56,48},{64,56},{72,6... | collective-permute-start | bytes 196616 | tf_op jit(solution)/shard_map/ppermute | solution.py:264
  3.8 6.5 %collective-permute-start = (bf16[128,256]{1,0:T(8,128)(2,1)}, bf16[128,256]{1,0:T(8,128)(2,1)S(1)}, u32[]{:S(2)}, u32[]{:S(2)}) collective-permute-start(bf16[128,256]{1,0:T(8,128)(2,1)} %bitcast.13), channel_id=1, source_target_pairs={{0,8},{8,16},{16,24},{24,32},{32,40},{40,48},{48,56},{56,64},{64,7... | collective-permute-start | bytes 196616 | tf_op jit(solution)/shard_map/ppermute | solution.py:263
  10.3 1.3 %slots.1 = (bf16[2048,384]{1,0:T(8,128)(2,1)S(1)}, f32[128,16]{1,0:T(8,128)S(1)}, s32[16,128]{1,0:T(8,128)S(1)}, bf16[128,256]{1,0:T(8,128)(2,1)S(1)}, bf16[128,...) custom-call(s32[1]{0:T(128)} %bitcast.2.first_row, s32[16,128]{1,0:T(8,128)} %bitcast.16, ...), custom_call_target="tpu_custom_call" | custom-call | tf_op jit(solution)/shard_map/slots/pallas_call | solution.py:272
  11.6 0.0 collective-permute-done.1.right
  11.6 0.3 collective-permute-done.left
  11.9 2.0 %shard_map.119 = (bf16[128,256]{1,0:T(8,128)(2,1)S(1)}, bf16[8,2,16,256]{3,2,1,0:T(8,128)(2,1)S(1)}, bf16[2048,256]{1,0:T(8,128)(2,1)S(1)}) custom-call(bf16[128,256]{1,0:T(8,128)(2,1)S(1)} %collective-permute-done.left, bf16[128,256]{1,0:T(8,128)(2,1)S(1)} %get-tuple-element.28.own, bf16[128,256]{1,0:T(8,128)(2,1)S(1)} %collective-permute-done.1.right, ...), custom_call_target="tpu_custom_call" | custom-call | tf_op jit(solution)/shard_map/pallas_call | solution.py:38
  13.9 20.3 %all_to_all.25.got = bf16[8,2,16,256]{3,2,1,0:T(8,128)(2,1)S(1)} all-to-all(bf16[8,2,16,256]{3,2,1,0:T(8,128)(2,1)S(1)} %get-tuple-element.34), channel_id=1, replica_groups=mesh['zl'=2,'x'=4,'y'=8,'zh'=4,'c'=2] {'zh','c'}, dimensions={0} | all-to-all | bytes 262144 | tf_op jit(solution)/shard_map/all_to_all | solution.py:253
  34.2 0.0 copy-done.1
  34.2 0.0 copy-done
  34.2 2.1 %shard_map.120 = (bf16[8,16,256]{2,1,0:T(8,128)(2,1)}, bf16[1536,128]{1,0:T(8,128)(2,1)S(1)}, bf16[512,128]{1,0:T(8,128)(2,1)S(1)}) custom-call(bf16[8,2,16,256]{3,2,1,0:T(8,128)(2,1)S(1)} %all_to_all.25.got, bf16[256,768]{1,0:T(8,128)(2,1)S(1)} %copy-done, bf16[256,256]{1,0:T(8,128)(2,1)S(1)} %copy-done.1), custom_call_target="tpu_custom_call" | custom-call | tf_op jit(solution)/shard_map/pallas_call | solution.py:38
  36.3 4.1 %all-to-all-start.1 = ((bf16[8,16,256]{2,1,0:T(8,128)(2,1)}), bf16[8,16,256]{2,1,0:T(8,128)(2,1)S(1)}, u32[]{:S(2)}, u32[]{:S(2)}) async-start(bf16[8,16,256]{2,1,0:T(8,128)(2,1)} %get-tuple-element.35), calls=%async_computation.1 | async-start | bytes 131072 | tf_op jit(solution)/shard_map/all_to_all | solution.py:253
  40.4 7.3 %all-to-all-done.1 = bf16[8,16,256]{2,1,0:T(8,128)(2,1)S(1)} async-done(((bf16[8,16,256]{2,1,0:T(8,128)(2,1)}), bf16[8,16,256]{2,1,0:T(8,128)(2,1)S(1)}, u32[]{:S(2)}, u32[]{:S(2)}) %all-to-all-start.1) | async-done | bytes 65568 | tf_op jit(solution)/shard_map/all_to_all | solution.py:253
  47.7 1.7 %shard_map.121 = (bf16[128,256]{1,0:T(8,128)(2,1)S(1)}, bf16[128,256]{1,0:T(8,128)(2,1)S(1)}, f32[128,256]{1,0:T(8,128)S(1)}, f32[128,256]{1,0:T(8,128)S(1)}, bf...) custom-call(s32[1]{0:T(128)} %bitcast.core, bf16[128,256]{1,0:T(8,128)(2,1)S(1)} %bitcast.9, ...), custom_call_target="tpu_custom_call" | custom-call | tf_op jit(solution)/shard_map/pallas_call | solution.py:38
  49.3 2.9 %all_gather.6.both = bf16[2,1536,128]{2,1,0:T(8,128)(2,1)S(1)} all-gather(bf16[1,1536,128]{2,1,0:T(8,128)(2,1)S(1)} %get-tuple-element.46), channel_id=1, replica_groups=mesh['zl'=2,'x'=4,'y'=8,'zh'=4,'c'=2] {'c'}, dimensions={0}, use_global_device_ids=true | all-gather | bytes 1179648 | tf_op jit(solution)/shard_map/all_gather | solution.py:326
  52.3 0.1 shard_map.123
  52.4 16.2 %all_to_all.26.parts = bf16[16,96,128]{2,1,0:T(8,128)(2,1)S(1)} all-to-all(bf16[16,96,128]{2,1,0:T(8,128)(2,1)S(1)} %shard_map.123), channel_id=1, replica_groups=mesh['zl'=2,'x'=4,'y'=8,'zh'=4,'c'=2] {'zl','y'}, dimensions={0} | all-to-all | bytes 786432 | tf_op jit(solution)/shard_map/all_to_all | solution.py:253
  68.6 0.1 shard_map.124
  68.7 17.6 %all_to_all.27.parts = bf16[16,96,128]{2,1,0:T(8,128)(2,1)S(1)} all-to-all(bf16[16,96,128]{2,1,0:T(8,128)(2,1)S(1)} %shard_map.124), channel_id=1, replica_groups=mesh['zl'=2,'x'=4,'y'=8,'zh'=4,'c'=2] {'x','zh'}, dimensions={0} | all-to-all | bytes 786432 | tf_op jit(solution)/shard_map/all_to_all | solution.py:253
  86.3 0.8 shard_map.125
  87.1 6.4 %all-to-all-start.4 = ((bf16[16,96,128]{2,1,0:T(8,128)(2,1)}), bf16[16,96,128]{2,1,0:T(8,128)(2,1)S(1)}, u32[]{:S(2)}, u32[]{:S(2)}) async-start(bf16[16,96,128]{2,1,0:T(8,128)(2,1)} %shard_map.125), calls=%async_computation.4 | async-start | bytes 786432 | tf_op jit(solution)/shard_map/all_to_all | solution.py:253
  93.6 4.9 %collective-permute-start.2 = (bf16[128,256]{1,0:T(8,128)(2,1)S(1)}, bf16[128,256]{1,0:T(8,128)(2,1)S(1)}, u32[]{:S(2)}, u32[]{:S(2)}) collective-permute-start(bf16[128,256]{1,0:T(8,128)(2,1)S(1)} %get-tuple-element.43), channel_id=1, source_target_pairs={{0,8},{8,16},{16,24},{24,32},{32,40},{40,48},{48,56},{56,64},{64,7... | collective-permute-start | bytes 196616 | tf_op jit(solution)/shard_map/ppermute | solution.py:321
  98.4 1.9 %collective-permute-start.3 = (bf16[128,256]{1,0:T(8,128)(2,1)S(1)}, bf16[128,256]{1,0:T(8,128)(2,1)S(1)}, u32[]{:S(2)}, u32[]{:S(2)}) collective-permute-start(bf16[128,256]{1,0:T(8,128)(2,1)S(1)} %get-tuple-element.44), channel_id=1, source_target_pairs={{8,0},{16,8},{24,16},{32,24},{40,32},{48,40},{56,48},{64,56},{72,6... | collective-permute-start | bytes 196616 | tf_op jit(solution)/shard_map/ppermute | solution.py:322
  100.4 2.4 %collective-permute-done.2.from_left = bf16[128,256]{1,0:T(8,128)(2,1)S(1)} collective-permute-done((bf16[128,256]{1,0:T(8,128)(2,1)S(1)}, bf16[128,256]{1,0:T(8,128)(2,1)S(1)}, u32[]{:S(2)}, u32[]{:S(2)}) %collective-permute-start.2) | collective-permute-done | bytes 65568 | tf_op jit(solution)/shard_map/ppermute | solution.py:321
  102.8 5.3 %collective-permute-done.3.from_right = bf16[128,256]{1,0:T(8,128)(2,1)S(1)} collective-permute-done((bf16[128,256]{1,0:T(8,128)(2,1)S(1)}, bf16[128,256]{1,0:T(8,128)(2,1)S(1)}, u32[]{:S(2)}, u32[]{:S(2)}) %collective-permute-start.3) | collective-permute-done | bytes 65568 | tf_op jit(solution)/shard_map/ppermute | solution.py:322
  108.1 0.8 shard_map.122
  108.9 0.0 all-to-all-done.4
  108.9 5.5 %all_gather.7.refs_0_ = bf16[2,1536,128]{2,1,0:T(8,128)(2,1)S(1)} all-gather(bf16[1,1536,128]{2,1,0:T(8,128)(2,1)S(1)} %bitcast.10), channel_id=1, replica_groups=mesh['zl'=2,'x'=4,'y'=8,'zh'=4,'c'=2] {'c'}, dimensions={0}, use_global_device_ids=true | all-gather | bytes 1179648 | tf_op jit(solution)/shard_map/all_gather | solution.py:336
  114.5 1.2 %shard_map.126 = (f32[256,256]{1,0:T(8,128)}, f32[256,256]{1,0:T(8,128)}, f32[256,768]{1,0:T(8,128)}, f32[256,256]{1,0:T(8,128)}) custom-call(bf16[2,1536,128]{2,1,0:T(8,128)(2,1)S(1)} %all_gather.7.refs_0_), custom_call_target="tpu_custom_call" | custom-call | tf_op jit(solution)/shard_map/pallas_call | solution.py:38
Async XLA Ops:
  0.6 33.5 %copy-start.1 = (bf16[256,256]{1,0:T(8,128)(2,1)S(1)}, bf16[256,256]{1,0:T(8,128)(2,1)}, u32[]{:S(2)}) copy-start(bf16[256,256]{1,0:T(8,128)(2,1)} %oproj.1) | copy-start | bytes 393220
  0.6 33.5 %copy-start = (bf16[256,768]{1,0:T(8,128)(2,1)S(1)}, bf16[256,768]{1,0:T(8,128)(2,1)}, u32[]{:S(2)}) copy-start(bf16[256,768]{1,0:T(8,128)(2,1)} %aproj.1) | copy-start | bytes 1179652
  0.7 10.9 %collective-permute-start.1 = (bf16[128,256]{1,0:T(8,128)(2,1)}, bf16[128,256]{1,0:T(8,128)(2,1)S(1)}, u32[]{:S(2)}, u32[]{:S(2)}) collective-permute-start(bf16[128,256]{1,0:T(8,128)(2,1)} %bitcast.12), channel_id=1, source_target_pairs={{8,0},{16,8},{24,16},{32,24},{40,32},{48,40},{56,48},{64,56},{72,6... | collective-permute-start | bytes 196616 | tf_op jit(solution)/shard_map/ppermute | solution.py:264
  3.8 8.2 %collective-permute-start = (bf16[128,256]{1,0:T(8,128)(2,1)}, bf16[128,256]{1,0:T(8,128)(2,1)S(1)}, u32[]{:S(2)}, u32[]{:S(2)}) collective-permute-start(bf16[128,256]{1,0:T(8,128)(2,1)} %bitcast.13), channel_id=1, source_target_pairs={{0,8},{8,16},{16,24},{24,32},{32,40},{40,48},{48,56},{56,64},{64,7... | collective-permute-start | bytes 196616 | tf_op jit(solution)/shard_map/ppermute | solution.py:263
  36.3 11.4 %all-to-all-start.1 = ((bf16[8,16,256]{2,1,0:T(8,128)(2,1)}), bf16[8,16,256]{2,1,0:T(8,128)(2,1)S(1)}, u32[]{:S(2)}, u32[]{:S(2)}) async-start(bf16[8,16,256]{2,1,0:T(8,128)(2,1)} %get-tuple-element.35), calls=%async_computation.1 | async-start | bytes 131072 | tf_op jit(solution)/shard_map/all_to_all | solution.py:253
  87.1 21.8 %all-to-all-start.4 = ((bf16[16,96,128]{2,1,0:T(8,128)(2,1)}), bf16[16,96,128]{2,1,0:T(8,128)(2,1)S(1)}, u32[]{:S(2)}, u32[]{:S(2)}) async-start(bf16[16,96,128]{2,1,0:T(8,128)(2,1)} %shard_map.125), calls=%async_computation.4 | async-start | bytes 786432 | tf_op jit(solution)/shard_map/all_to_all | solution.py:253
  93.6 9.2 %collective-permute-start.2 = (bf16[128,256]{1,0:T(8,128)(2,1)S(1)}, bf16[128,256]{1,0:T(8,128)(2,1)S(1)}, u32[]{:S(2)}, u32[]{:S(2)}) collective-permute-start(bf16[128,256]{1,0:T(8,128)(2,1)S(1)} %get-tuple-element.43), channel_id=1, source_target_pairs={{0,8},{8,16},{16,24},{24,32},{32,40},{40,48},{48,56},{56,64},{64,7... | collective-permute-start | bytes 196616 | tf_op jit(solution)/shard_map/ppermute | solution.py:321
  98.4 9.7 %collective-permute-start.3 = (bf16[128,256]{1,0:T(8,128)(2,1)S(1)}, bf16[128,256]{1,0:T(8,128)(2,1)S(1)}, u32[]{:S(2)}, u32[]{:S(2)}) collective-permute-start(bf16[128,256]{1,0:T(8,128)(2,1)S(1)} %get-tuple-element.44), channel_id=1, source_target_pairs={{8,0},{16,8},{24,16},{32,24},{40,32},{48,40},{56,48},{64,56},{72,6... | collective-permute-start | bytes 196616 | tf_op jit(solution)/shard_map/ppermute | solution.py:322

commit v3 on v2

--- a/solution.py
+++ b/solution.py
@@ -17,12 +17,12 @@
 SLOTS = 16
 LANES = 128
 
-FINE = (2, 4, 8, 4, 2)
-FINE_NAMES = ("zl", "x", "y", "zh", "c")
-DOM = ("zl", "x", "y")
+FINE = (2, 4, 4, 2, 4, 2)
+FINE_NAMES = ("zl", "x", "yh", "yl", "zh", "c")
+DOM = ("zl", "x", "yh", "yl")
 SNAP = ("zh", "c")
-SCATTER = ("zl", "y")
-ACROSS = ("x", "zh")
+SCATTER = ("zl", "x", "yl")
+ACROSS = ("yh", "zh")
 
 f32 = jnp.float32
 bf16 = jnp.bfloat16
@@ -120,7 +120,7 @@
         sent[s, 1] = cot[s * share : (s + 1) * share]
 
 
-def temporal_kernel(got, aproj, oproj, grad_spatial, attend_out, output_out, prods, sums):
+def temporal_kernel(got, aproj, oproj, grad_spatial, att_out, three, prods, sums):
     snaps, _, nodes, _ = got.shape
     rows = snaps * nodes
     x = got[:, 0].reshape(rows, WIDTH)
@@ -166,8 +166,7 @@
         grad_query.append(jnp.sum(grad_score * key3, axis=0) * inverse_root)
         grad_key = grad_key + grad_score * qs[one][None]
         grad_val = grad_val + soft * da[one][None]
-    att = jnp.concatenate(attended, axis=0).astype(bf16)
-    put_slab(output_out, 0, mm_tn(att, c))
+    att_out[...] = jnp.concatenate(attended, axis=0).astype(bf16)
     parts = (
         jnp.concatenate(grad_query, axis=0).astype(bf16),
         grad_key.reshape(rows, WIDTH).astype(bf16),
@@ -175,14 +174,31 @@
     )
     total = c.astype(f32)
     for p, part in enumerate(parts):
-        put_slab(attend_out, p, mm_tn(x, part))
+        three[p] = part
         total = total + mm_nt(part, aproj[:, p * WIDTH : (p + 1) * WIDTH])
     grad_spatial[...] = total.astype(bf16).reshape(snaps, nodes, WIDTH)
 
 
+def halves(core, first, second, keep, send):
+    mine = core[0] == 0
+    for n, (a, b) in enumerate(zip(first, second)):
+        a = a.astype(bf16)
+        b = b.astype(bf16)
+        put_slab(keep, n, jnp.where(mine, a, b))
+        put_slab(send.at[0], n, jnp.where(mine, b, a))
+
+
+def products_kernel(core, got, att, three, keep, send):
+    snaps, _, nodes, _ = got.shape
+    x = got[:, 0].reshape(snaps * nodes, WIDTH)
+    c = got[:, 1].reshape(snaps * nodes, WIDTH)
+    attend = [mm_tn(x, three[p]) for p in range(3)]
+    halves(core, attend[:2], (attend[2], mm_tn(att[...], c)), keep, send)
+
+
 def backward_kernel(
-    core, gs_ref, comb, slopew, nbrt, left, own, right, cproj, att_in, out_in,
-    to_left, to_right, own_rows, base, keep, send, gb, other, hot
+    core, gs_ref, comb, slopew, nbrt, left, own, right, cproj,
+    to_left, to_right, own_rows, base, keep, send, gb, hot
 ):
     rows = own.shape[0]
     gs = gs_ref[...]
@@ -204,12 +220,7 @@
     message = mm_tn(left[...], rounded[:HALO])
     message = message + mm_tn(own[...], rounded[HALO : HALO + rows])
     message = message + mm_tn(right[...], rounded[HALO + rows :])
-    other[: 2 * WIDTH] = out_in[...]
-    put_slab(other, 1, message)
-    put_slab(other, 2, mm_tn(comb[...], gs))
-    first = core[0] == 0
-    keep[...] = jnp.where(first, att_in[...], other[...])
-    send[0] = jnp.where(first, other[...], att_in[...])
+    halves(core, (message,), (mm_tn(comb[...], gs),), keep, send)
 
 
 def features_kernel(base, own_rows, from_left, from_right, mproj, grad):
@@ -217,9 +228,15 @@
     grad[...] = (base[...] + mm_nt(own.astype(bf16), mproj[...])).astype(bf16)
 
 
-def pair_kernel(core, keep, both, out):
-    other = jnp.where(core[0] == 0, both[1], both[0])
-    out[...] = (keep[...].astype(f32) + other.astype(f32)).astype(bf16).reshape(out.shape)
+def pair_kernel(core, early, early_both, late, late_both, out):
+    mine = core[0] == 0
+
+    def total(keep, both):
+        other = jnp.where(mine, both[1], both[0])
+        return (keep[...].astype(f32) + other.astype(f32)).astype(bf16)
+
+    value = jnp.concatenate([total(early, early_both), total(late, late_both)], axis=0)
+    out[...] = value.reshape(out.shape)
 
 
 def fold_kernel(parts, out):
@@ -242,10 +259,11 @@
         ref[:, at : at + LANES] = pair[0]
         ref[:, at + LANES : at + 2 * LANES] = pair[1]
 
-    for p in range(3):
-        put(attend, p * WIDTH, get(0, p))
-    put(output, 0, get(1, 0))
-    put(message, 0, get(1, 1))
+    put(attend, 0, get(0, 0))
+    put(attend, WIDTH, get(0, 1))
+    put(attend, 2 * WIDTH, get(1, 0))
+    put(output, 0, get(1, 1))
+    put(message, 0, get(0, 2))
     put(combine, 0, get(1, 2))
 
 
@@ -297,13 +315,20 @@
         [pltpu.VMEM((3 * HALO, width), bf16)],
     )
     got = swap(sent, SNAP)
-    grads, attend_part, output_part = call(
+    grads, att, three = call(
         temporal_kernel,
-        [((SNAPS, rows // SNAPS, width), bf16), ((6 * width, LANES), bf16), ((2 * width, LANES), bf16)],
+        [((SNAPS, rows // SNAPS, width), bf16), ((rows, width), bf16), ((3, rows, width), bf16)],
         (got, aproj, oproj),
         [pltpu.VMEM((2 * SNAPS * rows, 2 * width), bf16), pltpu.VMEM((2 * SNAPS * rows, width), f32)],
     )
     grad_spatial = swap(grads, SNAP).reshape(rows, width)
+    early, send = call(
+        products_kernel,
+        [((4 * width, LANES), bf16), ((1, 4 * width, LANES), bf16)],
+        (core, got, att, three),
+        scalars=1,
+    )
+    early_both = lax.all_gather(send, "c", axis=0, tiled=True)
     to_left, to_right, own_rows, base, keep, send = call(
         backward_kernel,
         [
@@ -311,23 +336,31 @@
             ((HALO, width), bf16),
             ((rows, width), f32),
             ((rows, width), f32),
-            ((6 * width, LANES), bf16),
-            ((1, 6 * width, LANES), bf16),
+            ((2 * width, LANES), bf16),
+            ((1, 2 * width, LANES), bf16),
         ],
-        (core, grad_spatial, combined, slopew, nbrt, from_left, own, from_right, cproj, attend_part, output_part),
-        [pltpu.VMEM((edges, width), bf16), pltpu.VMEM((6 * width, LANES), bf16), pltpu.VMEM((3 * HALO, edges), bf16)],
+        (core, grad_spatial, combined, slopew, nbrt, from_left, own, from_right, cproj),
+        [pltpu.VMEM((edges, width), bf16), pltpu.VMEM((3 * HALO, edges), bf16)],
         scalars=1,
     )
     back_left = lax.ppermute(to_right, DOM, up)
     back_right = lax.ppermute(to_left, DOM, down)
     (grad_features,) = call(
-        features_kernel, [((rows, width), bf16)], (base, own_rows, back_left, back_right, mproj), stored=True
-    )
-    both = lax.all_gather(send, "c", axis=0, tiled=True)
+        features_kernel,
+        [((rows, width), bf16)],
+        (base, own_rows, back_left, back_right, mproj),
+        stored=True,
+    )
+    late_both = lax.all_gather(send, "c", axis=0, tiled=True)
     count = lax.axis_size(SCATTER)
     across = lax.axis_size(ACROSS)
     piece = 6 * width // count
-    (mine,) = call(pair_kernel, [((count, piece, LANES), bf16)], (core, keep, both), scalars=1)
+    (mine,) = call(
+        pair_kernel,
+        [((count, piece, LANES), bf16)],
+        (core, early, early_both, keep, late_both),
+        scalars=1,
+    )
     parts = swap(mine, SCATTER)
     (spread,) = call(fold_kernel, [((across, piece, LANES), bf16)], (parts,))
     parts = swap(spread, ACROSS)

time: 116 us -> 112 us (0.966)
  blocking collectives: 62.6 us -> 39.3 us
  starting transfers between devices: 27 us -> 40.1 us
  waiting for transfers between devices: 15.3 us -> 20.7 us
    all_to_all x3 -> x2, blocking collectives: 54.1 us -> 29.8 us  [swap(): return lax.all_to_all(x, axes, split_axis=0, concat_axis=0, tiled=True)]
    all_to_all x2 -> x3, starting transfers between devices: 10.5 us -> 24.6 us  [swap(): return lax.all_to_all(x, axes, split_axis=0, concat_axis=0, tiled=True)]
    all_to_all x2 -> x3, waiting for transfers between devices: 7.28 us -> 13.1 us  [swap(): return lax.all_to_all(x, axes, split_axis=0, concat_axis=0, tiled=True)]
    ppermute x1, waiting for transfers between devices: 2.42 us -> 0.16 us  [step(): back_left = lax.ppermute(to_right, DOM, up)]
    ppermute x1, waiting for transfers between devices: 5.33 us -> 7.14 us  [step(): back_right = lax.ppermute(to_left, DOM, down)]
    all_gather x1 -> x2, blocking collectives: 2.95 us -> 4.76 us  [the longest x1 2.58 us: step(): late_both = lax.all_gather(send, 'c', axis=0, tiled=True)]
    pallas_call x8 -> x9, Pallas kernels: 8.72 us -> 9.55 us  [call(): pl.pallas_call(kernel, out_shape=[place(s, d) for s, d in outs], in_specs...]
  transfers between devices with their start and end apart: 6 -> 7, of which waited for: 4 -> 5; matrix products, arithmetic and copies ran while one was open for 0% -> 0% of each run, Pallas kernels for 2% -> 2%
where the time goes in v3:
time: 112 us
  starting transfers between devices  40.1 us (36%)
  blocking collectives  39.3 us (35%)
  waiting for transfers between devices  20.7 us (18%)
  Pallas kernels  10.8 us (10%)
    all_to_all x2, blocking collectives, swap(): return lax.all_to_all(x, axes, split_axis=0, concat_axis=0, tiled=True)  29.8 us
    all_to_all x3, starting transfers between devices, swap(): return lax.all_to_all(x, axes, split_axis=0, concat_axis=0, tiled=True)  24.6 us
    all_to_all x3, waiting for transfers between devices, swap(): return lax.all_to_all(x, axes, split_axis=0, concat_axis=0, tiled=True)  13.1 us
    pallas_call x9, Pallas kernels, call(): pl.pallas_call(kernel, out_shape=[place(s, d) for s, d in outs], in_specs...  9.55 us
    ppermute x1, waiting for transfers between devices, step(): back_right = lax.ppermute(to_left, DOM, down)  7.14 us
    ppermute x1, starting transfers between devices, step(): from_left = lax.ppermute(own, DOM, up)  6.52 us
    all_gather x1, blocking collectives, step(): sums = lax.all_gather(half, 'c', axis=0, tiled=True)  4.79 us
    ppermute x1, starting transfers between devices, step(): back_left = lax.ppermute(to_right, DOM, up)  3.9 us
  transfers between devices with their start and end apart: 7, of which 5 were waited for; matrix products, arithmetic and copies ran while one was open for 0% of the time, Pallas kernels for 2%

profile of v3, /device:TPU:63, one launch (start us, length us, event | category | flops | bytes accessed | tf_op | source)
XLA Modules:
  0.0 111.7 jit_solution(12507483926931757356)
XLA Ops:
  0.6 0.0 copy-start.1
  0.6 0.0 copy-start
  0.7 3.1 %collective-permute-start.1 = (bf16[128,256]{1,0:T(8,128)(2,1)}, bf16[128,256]{1,0:T(8,128)(2,1)S(1)}, u32[]{:S(2)}, u32[]{:S(2)}) collective-permute-start(bf16[128,256]{1,0:T(8,128)(2,1)} %bitcast.12), channel_id=1, source_target_pairs={{8,0},{16,8},{24,16},{32,24},{40,32},{48,40},{56,48},{64,56},{72,6... | collective-permute-start | bytes 196616 | tf_op jit(solution)/shard_map/ppermute | solution.py:282
  3.8 6.5 %collective-permute-start = (bf16[128,256]{1,0:T(8,128)(2,1)}, bf16[128,256]{1,0:T(8,128)(2,1)S(1)}, u32[]{:S(2)}, u32[]{:S(2)}) collective-permute-start(bf16[128,256]{1,0:T(8,128)(2,1)} %bitcast.13), channel_id=1, source_target_pairs={{0,8},{8,16},{16,24},{24,32},{32,40},{40,48},{48,56},{56,64},{64,7... | collective-permute-start | bytes 196616 | tf_op jit(solution)/shard_map/ppermute | solution.py:281
  10.3 1.3 %slots.1 = (bf16[2048,384]{1,0:T(8,128)(2,1)S(1)}, f32[128,16]{1,0:T(8,128)S(1)}, s32[16,128]{1,0:T(8,128)S(1)}, bf16[128,256]{1,0:T(8,128)(2,1)S(1)}, bf16[128,...) custom-call(s32[1]{0:T(128)} %bitcast.2.first_row, s32[16,128]{1,0:T(8,128)} %bitcast.16, ...), custom_call_target="tpu_custom_call" | custom-call | tf_op jit(solution)/shard_map/slots/pallas_call | solution.py:290
  11.6 0.0 collective-permute-done.1.right
  11.6 0.3 collective-permute-done.left
  11.9 2.6 %shard_map.119 = (bf16[128,256]{1,0:T(8,128)(2,1)S(1)}, bf16[8,2,16,256]{3,2,1,0:T(8,128)(2,1)}, bf16[2048,256]{1,0:T(8,128)(2,1)S(1)}) custom-call(bf16[128,256]{1,0:T(8,128)(2,1)S(1)} %collective-permute-done.left, bf16[128,256]{1,0:T(8,128)(2,1)S(1)} %get-tuple-element.30.own, bf16[128,256]{1,0:T(8,128)(2,1)S(1)} %collective-permute-done.1.right, ...), custom_call_target="tpu_custom_call" | custom-call | tf_op jit(solution)/shard_map/pallas_call | solution.py:38
  14.6 12.1 %all-to-all-start = ((bf16[8,2,16,256]{3,2,1,0:T(8,128)(2,1)}), bf16[8,2,16,256]{3,2,1,0:T(8,128)(2,1)S(1)}, u32[]{:S(2)}, u32[]{:S(2)}) async-start(bf16[8,2,16,256]{3,2,1,0:T(8,128)(2,1)} %get-tuple-element.36), calls=%async_computation | async-start | bytes 262144 | tf_op jit(solution)/shard_map/all_to_all | solution.py:271
  26.7 8.3 %all-to-all-done.got = bf16[8,2,16,256]{3,2,1,0:T(8,128)(2,1)S(1)} async-done(((bf16[8,2,16,256]{3,2,1,0:T(8,128)(2,1)}), bf16[8,2,16,256]{3,2,1,0:T(8,128)(2,1)S(1)}, u32[]{:S(2)}, u32[]{:S(2)}) %all-to-all-start) | async-done | bytes 131104 | tf_op jit(solution)/shard_map/all_to_all | solution.py:271
  35.0 0.0 copy-done.1
  35.0 2.0 %shard_map.120 = (bf16[8,16,256]{2,1,0:T(8,128)(2,1)}, bf16[128,256]{1,0:T(8,128)(2,1)S(1)}, bf16[3,128,256]{2,1,0:T(8,128)(2,1)S(1)}) custom-call(bf16[8,2,16,256]{3,2,1,0:T(8,128)(2,1)S(1)} %all-to-all-done.got, bf16[256,768]{1,0:T(8,128)(2,1)S(1)} %copy-done, bf16[256,256]{1,0:T(8,128)(2,1)S(1)} %copy-done.1), custom_call_target="tpu_custom_call" | custom-call | tf_op jit(solution)/shard_map/pallas_call | solution.py:38
  37.1 4.1 %all-to-all-start.1 = ((bf16[8,16,256]{2,1,0:T(8,128)(2,1)}), bf16[8,16,256]{2,1,0:T(8,128)(2,1)S(1)}, u32[]{:S(2)}, u32[]{:S(2)}) async-start(bf16[8,16,256]{2,1,0:T(8,128)(2,1)} %get-tuple-element.37), calls=%async_computation.1 | async-start | bytes 131072 | tf_op jit(solution)/shard_map/all_to_all | solution.py:271
  41.2 0.3 shard_map.123
  41.5 2.2 %all_gather.9.early_both = bf16[2,1024,128]{2,1,0:T(8,128)(2,1)S(1)} all-gather(bf16[1,1024,128]{2,1,0:T(8,128)(2,1)S(1)} %get-tuple-element.48), channel_id=1, replica_groups=mesh['zl'=2,'x'=4,'yh'=4,'yl'=2,'zh'=4,'c'=2] {'c'}, dimensions={0}, use_global_device_ids=true | all-gather | bytes 786432 | tf_op jit(solution)/shard_map/all_gather | solution.py:331
  43.7 4.8 %all-to-all-done.1 = bf16[8,16,256]{2,1,0:T(8,128)(2,1)S(1)} async-done(((bf16[8,16,256]{2,1,0:T(8,128)(2,1)}), bf16[8,16,256]{2,1,0:T(8,128)(2,1)S(1)}, u32[]{:S(2)}, u32[]{:S(2)}) %all-to-all-start.1) | async-done | bytes 65568 | tf_op jit(solution)/shard_map/all_to_all | solution.py:271
  48.4 1.6 %shard_map.121 = (bf16[128,256]{1,0:T(8,128)(2,1)S(1)}, bf16[128,256]{1,0:T(8,128)(2,1)S(1)}, f32[128,256]{1,0:T(8,128)S(1)}, f32[128,256]{1,0:T(8,128)S(1)}, bf...) custom-call(s32[1]{0:T(128)} %bitcast.core, bf16[128,256]{1,0:T(8,128)(2,1)S(1)} %bitcast.9, ...), custom_call_target="tpu_custom_call" | custom-call | tf_op jit(solution)/shard_map/pallas_call | solution.py:38
  50.0 2.6 %all_gather.10.late_both = bf16[2,512,128]{2,1,0:T(8,128)(2,1)S(1)} all-gather(bf16[1,512,128]{2,1,0:T(8,128)(2,1)S(1)} %get-tuple-element.50), channel_id=1, replica_groups=mesh['zl'=2,'x'=4,'yh'=4,'yl'=2,'zh'=4,'c'=2] {'c'}, dimensions={0}, use_global_device_ids=true | all-gather | bytes 393216 | tf_op jit(solution)/shard_map/all_gather | solution.py:354
  52.6 0.1 shard_map.124
  52.7 10.5 %all_to_all.25.parts = bf16[16,96,128]{2,1,0:T(8,128)(2,1)S(1)} all-to-all(bf16[16,96,128]{2,1,0:T(8,128)(2,1)S(1)} %shard_map.124), channel_id=1, replica_groups=mesh['zl'=2,'x'=4,'yh'=4,'yl'=2,'zh'=4,'c'=2] {'zl','x','yl'}, dimensions={0} | all-to-all | bytes 786432 | tf_op jit(solution)/shard_map/all_to_all | solution.py:271
  63.2 0.1 shard_map.125
  63.3 19.3 %all_to_all.26.parts = bf16[16,96,128]{2,1,0:T(8,128)(2,1)S(1)} all-to-all(bf16[16,96,128]{2,1,0:T(8,128)(2,1)S(1)} %shard_map.125), channel_id=1, replica_groups=mesh['zl'=2,'x'=4,'yh'=4,'yl'=2,'zh'=4,'c'=2] {'yh','zh'}, dimensions={0} | all-to-all | bytes 786432 | tf_op jit(solution)/shard_map/all_to_all | solution.py:271
  82.6 0.8 shard_map.126
  83.4 8.4 %all-to-all-start.4 = ((bf16[16,96,128]{2,1,0:T(8,128)(2,1)}), bf16[16,96,128]{2,1,0:T(8,128)(2,1)S(1)}, u32[]{:S(2)}, u32[]{:S(2)}) async-start(bf16[16,96,128]{2,1,0:T(8,128)(2,1)} %shard_map.126), calls=%async_computation.4 | async-start | bytes 786432 | tf_op jit(solution)/shard_map/all_to_all | solution.py:271
  91.8 3.9 %collective-permute-start.2 = (bf16[128,256]{1,0:T(8,128)(2,1)S(1)}, bf16[128,256]{1,0:T(8,128)(2,1)S(1)}, u32[]{:S(2)}, u32[]{:S(2)}) collective-permute-start(bf16[128,256]{1,0:T(8,128)(2,1)S(1)} %get-tuple-element.43), channel_id=1, source_target_pairs={{0,8},{8,16},{16,24},{24,32},{32,40},{40,48},{48,56},{56,64},{64,7... | collective-permute-start | bytes 196616 | tf_op jit(solution)/shard_map/ppermute | solution.py:346
  95.7 1.9 %collective-permute-start.3 = (bf16[128,256]{1,0:T(8,128)(2,1)S(1)}, bf16[128,256]{1,0:T(8,128)(2,1)S(1)}, u32[]{:S(2)}, u32[]{:S(2)}) collective-permute-start(bf16[128,256]{1,0:T(8,128)(2,1)S(1)} %get-tuple-element.44), channel_id=1, source_target_pairs={{8,0},{16,8},{24,16},{32,24},{40,32},{48,40},{56,48},{64,56},{72,6... | collective-permute-start | bytes 196616 | tf_op jit(solution)/shard_map/ppermute | solution.py:347
  97.6 0.2 collective-permute-done.2.from_left
  97.8 7.1 %collective-permute-done.3.from_right = bf16[128,256]{1,0:T(8,128)(2,1)S(1)} collective-permute-done((bf16[128,256]{1,0:T(8,128)(2,1)S(1)}, bf16[128,256]{1,0:T(8,128)(2,1)S(1)}, u32[]{:S(2)}, u32[]{:S(2)}) %collective-permute-start.3) | collective-permute-done | bytes 65568 | tf_op jit(solution)/shard_map/ppermute | solution.py:347
  104.9 0.8 shard_map.122
  105.7 0.0 all-to-all-done.4
  105.7 4.8 %all_gather.11.refs_0_ = bf16[2,1536,128]{2,1,0:T(8,128)(2,1)S(1)} all-gather(bf16[1,1536,128]{2,1,0:T(8,128)(2,1)S(1)} %bitcast.10), channel_id=1, replica_groups=mesh['zl'=2,'x'=4,'yh'=4,'yl'=2,'zh'=4,'c'=2] {'c'}, dimensions={0}, use_global_device_ids=true | all-gather | bytes 1179648 | tf_op jit(solution)/shard_map/all_gather | solution.py:369
  110.5 1.2 %shard_map.127 = (f32[256,256]{1,0:T(8,128)}, f32[256,256]{1,0:T(8,128)}, f32[256,768]{1,0:T(8,128)}, f32[256,256]{1,0:T(8,128)}) custom-call(bf16[2,1536,128]{2,1,0:T(8,128)(2,1)S(1)} %all_gather.11.refs_0_), custom_call_target="tpu_custom_call" | custom-call | tf_op jit(solution)/shard_map/pallas_call | solution.py:38
  (1 shorter events, 0.0 us)
Async XLA Ops:
  0.6 34.4 %copy-start.1 = (bf16[256,256]{1,0:T(8,128)(2,1)S(1)}, bf16[256,256]{1,0:T(8,128)(2,1)}, u32[]{:S(2)}) copy-start(bf16[256,256]{1,0:T(8,128)(2,1)} %oproj.1) | copy-start | bytes 393220
  0.6 34.4 %copy-start = (bf16[256,768]{1,0:T(8,128)(2,1)S(1)}, bf16[256,768]{1,0:T(8,128)(2,1)}, u32[]{:S(2)}) copy-start(bf16[256,768]{1,0:T(8,128)(2,1)} %aproj.1) | copy-start | bytes 1179652
  0.7 10.9 %collective-permute-start.1 = (bf16[128,256]{1,0:T(8,128)(2,1)}, bf16[128,256]{1,0:T(8,128)(2,1)S(1)}, u32[]{:S(2)}, u32[]{:S(2)}) collective-permute-start(bf16[128,256]{1,0:T(8,128)(2,1)} %bitcast.12), channel_id=1, source_target_pairs={{8,0},{16,8},{24,16},{32,24},{40,32},{48,40},{56,48},{64,56},{72,6... | collective-permute-start | bytes 196616 | tf_op jit(solution)/shard_map/ppermute | solution.py:282
  3.8 8.2 %collective-permute-start = (bf16[128,256]{1,0:T(8,128)(2,1)}, bf16[128,256]{1,0:T(8,128)(2,1)S(1)}, u32[]{:S(2)}, u32[]{:S(2)}) collective-permute-start(bf16[128,256]{1,0:T(8,128)(2,1)} %bitcast.13), channel_id=1, source_target_pairs={{0,8},{8,16},{16,24},{24,32},{32,40},{40,48},{48,56},{56,64},{64,7... | collective-permute-start | bytes 196616 | tf_op jit(solution)/shard_map/ppermute | solution.py:281
  14.6 20.5 %all-to-all-start = ((bf16[8,2,16,256]{3,2,1,0:T(8,128)(2,1)}), bf16[8,2,16,256]{3,2,1,0:T(8,128)(2,1)S(1)}, u32[]{:S(2)}, u32[]{:S(2)}) async-start(bf16[8,2,16,256]{3,2,1,0:T(8,128)(2,1)} %get-tuple-element.36), calls=%async_computation | async-start | bytes 262144 | tf_op jit(solution)/shard_map/all_to_all | solution.py:271
  37.1 11.4 %all-to-all-start.1 = ((bf16[8,16,256]{2,1,0:T(8,128)(2,1)}), bf16[8,16,256]{2,1,0:T(8,128)(2,1)S(1)}, u32[]{:S(2)}, u32[]{:S(2)}) async-start(bf16[8,16,256]{2,1,0:T(8,128)(2,1)} %get-tuple-element.37), calls=%async_computation.1 | async-start | bytes 131072 | tf_op jit(solution)/shard_map/all_to_all | solution.py:271
  83.4 22.4 %all-to-all-start.4 = ((bf16[16,96,128]{2,1,0:T(8,128)(2,1)}), bf16[16,96,128]{2,1,0:T(8,128)(2,1)S(1)}, u32[]{:S(2)}, u32[]{:S(2)}) async-start(bf16[16,96,128]{2,1,0:T(8,128)(2,1)} %shard_map.126), calls=%async_computation.4 | async-start | bytes 786432 | tf_op jit(solution)/shard_map/all_to_all | solution.py:271
  91.8 6.0 %collective-permute-start.2 = (bf16[128,256]{1,0:T(8,128)(2,1)S(1)}, bf16[128,256]{1,0:T(8,128)(2,1)S(1)}, u32[]{:S(2)}, u32[]{:S(2)}) collective-permute-start(bf16[128,256]{1,0:T(8,128)(2,1)S(1)} %get-tuple-element.43), channel_id=1, source_target_pairs={{0,8},{8,16},{16,24},{24,32},{32,40},{40,48},{48,56},{56,64},{64,7... | collective-permute-start | bytes 196616 | tf_op jit(solution)/shard_map/ppermute | solution.py:346
  95.7 9.2 %collective-permute-start.3 = (bf16[128,256]{1,0:T(8,128)(2,1)S(1)}, bf16[128,256]{1,0:T(8,128)(2,1)S(1)}, u32[]{:S(2)}, u32[]{:S(2)}) collective-permute-start(bf16[128,256]{1,0:T(8,128)(2,1)S(1)} %get-tuple-element.44), channel_id=1, source_target_pairs={{8,0},{16,8},{24,16},{32,24},{40,32},{48,40},{56,48},{64,56},{72,6... | collective-permute-start | bytes 196616 | tf_op jit(solution)/shard_map/ppermute | solution.py:347

commit v4 on v3

--- a/solution.py
+++ b/solution.py
@@ -65,7 +65,7 @@
 
 
 def slots_kernel(
-    first_row, nbr_in, deg_in, own, cot, mproj, cproj,
+    place, nbr_in, deg_in, own, cot, mproj, cproj,
     hot, weights, nbrt, own_out, cot_out, mproj_out, cproj_out, table_in, deg, sems
 ):
     moves = ((nbr_in, table_in), (deg_in, deg), (own, own_out), (cot, cot_out), (mproj, mproj_out), (cproj, cproj_out))
@@ -75,7 +75,7 @@
     copies[0].wait()
     copies[1].wait()
     slots, rows = nbrt.shape
-    local = table_in[...] - first_row[0]
+    local = table_in[...] - ((place[0] >> 1) * rows - HALO)
     nbrt[...] = local
     pad = jnp.zeros((rows - slots - 1, rows), f32)
     table = jnp.concatenate([local.astype(f32), deg[...].astype(f32), pad], axis=0).T
@@ -179,8 +179,8 @@
     grad_spatial[...] = total.astype(bf16).reshape(snaps, nodes, WIDTH)
 
 
-def halves(core, first, second, keep, send):
-    mine = core[0] == 0
+def halves(place, first, second, keep, send):
+    mine = (place[0] & 1) == 0
     for n, (a, b) in enumerate(zip(first, second)):
         a = a.astype(bf16)
         b = b.astype(bf16)
@@ -188,16 +188,16 @@
         put_slab(send.at[0], n, jnp.where(mine, b, a))
 
 
-def products_kernel(core, got, att, three, keep, send):
+def products_kernel(place, got, att, three, keep, send):
     snaps, _, nodes, _ = got.shape
     x = got[:, 0].reshape(snaps * nodes, WIDTH)
     c = got[:, 1].reshape(snaps * nodes, WIDTH)
     attend = [mm_tn(x, three[p]) for p in range(3)]
-    halves(core, attend[:2], (attend[2], mm_tn(att[...], c)), keep, send)
+    halves(place, attend[:2], (attend[2], mm_tn(att[...], c)), keep, send)
 
 
 def backward_kernel(
-    core, gs_ref, comb, slopew, nbrt, left, own, right, cproj,
+    place, gs_ref, comb, slopew, nbrt, left, own, right, cproj,
     to_left, to_right, own_rows, base, keep, send, gb, hot
 ):
     rows = own.shape[0]
@@ -220,7 +220,7 @@
     message = mm_tn(left[...], rounded[:HALO])
     message = message + mm_tn(own[...], rounded[HALO : HALO + rows])
     message = message + mm_tn(right[...], rounded[HALO + rows :])
-    halves(core, (message,), (mm_tn(comb[...], gs),), keep, send)
+    halves(place, (message,), (mm_tn(comb[...], gs),), keep, send)
 
 
 def features_kernel(base, own_rows, from_left, from_right, mproj, grad):
@@ -228,8 +228,8 @@
     grad[...] = (base[...] + mm_nt(own.astype(bf16), mproj[...])).astype(bf16)
 
 
-def pair_kernel(core, early, early_both, late, late_both, out):
-    mine = core[0] == 0
+def pair_kernel(place, early, early_both, late, late_both, out):
+    mine = (place[0] & 1) == 0
 
     def total(keep, both):
         other = jnp.where(mine, both[1], both[0])
@@ -280,8 +280,7 @@
     cot = cotangent[0]
     from_left = lax.ppermute(own, DOM, up)
     from_right = lax.ppermute(own, DOM, down)
-    first_row = (lax.axis_index(DOM) * rows - HALO).reshape(1)
-    core = lax.axis_index("c").reshape(1)
+    where = (lax.axis_index(DOM) * 2 + lax.axis_index("c")).reshape(1)
     edges = SLOTS * rows
     stored = [
         pltpu.with_memory_space_constraint(a, pltpu.HBM)
@@ -307,7 +306,7 @@
         ],
         compiler_params=pltpu.CompilerParams(vmem_limit_bytes=24 * 2**20),
         name="slots",
-    )(first_row, *stored)
+    )(where, *stored)
     combined, sent, slopew = call(
         forward_kernel,
         [((rows, width), bf16), ((SNAPS, 2, rows // SNAPS, width), bf16), ((edges, width), bf16)],
@@ -325,7 +324,7 @@
     early, send = call(
         products_kernel,
         [((4 * width, LANES), bf16), ((1, 4 * width, LANES), bf16)],
-        (core, got, att, three),
+        (where, got, att, three),
         scalars=1,
     )
     early_both = lax.all_gather(send, "c", axis=0, tiled=True)
@@ -339,7 +338,7 @@
             ((2 * width, LANES), bf16),
             ((1, 2 * width, LANES), bf16),
         ],
-        (core, grad_spatial, combined, slopew, nbrt, from_left, own, from_right, cproj),
+        (where, grad_spatial, combined, slopew, nbrt, from_left, own, from_right, cproj),
         [pltpu.VMEM((edges, width), bf16), pltpu.VMEM((3 * HALO, edges), bf16)],
         scalars=1,
     )
@@ -358,7 +357,7 @@
     (mine,) = call(
         pair_kernel,
         [((count, piece, LANES), bf16)],
-        (core, early, early_both, keep, late_both),
+        (where, early, early_both, keep, late_both),
         scalars=1,
     )
     parts = swap(mine, SCATTER)

time: 112 us -> 111 us (level)
  blocking collectives: 39.3 us -> 59.6 us
  starting transfers between devices: 40.1 us -> 28 us
  waiting for transfers between devices: 20.7 us -> 12.4 us
    all_to_all x2 -> x3, blocking collectives: 29.8 us -> 50 us  [swap(): return lax.all_to_all(x, axes, split_axis=0, concat_axis=0, tiled=True)]
    all_to_all x3 -> x2, starting transfers between devices: 24.6 us -> 12.5 us  [swap(): return lax.all_to_all(x, axes, split_axis=0, concat_axis=0, tiled=True)]
    all_to_all x3 -> x2, waiting for transfers between devices: 13.1 us -> 4.76 us  [swap(): return lax.all_to_all(x, axes, split_axis=0, concat_axis=0, tiled=True)]
  transfers between devices with their start and end apart: 7 -> 6, of which waited for: 5 -> 4; matrix products, arithmetic and copies ran while one was open for 0% -> 0% of each run, Pallas kernels for 2% -> 2%
where the time goes in v4:
time: 111 us
  blocking collectives  59.6 us (54%)
  starting transfers between devices  28 us (25%)
  waiting for transfers between devices  12.4 us (11%)
  Pallas kernels  10.2 us (9%)
    all_to_all x3, blocking collectives, swap(): return lax.all_to_all(x, axes, split_axis=0, concat_axis=0, tiled=True)  50 us
    all_to_all x2, starting transfers between devices, swap(): return lax.all_to_all(x, axes, split_axis=0, concat_axis=0, tiled=True)  12.5 us
    pallas_call x9, Pallas kernels, call(): pl.pallas_call(kernel, out_shape=[place(s, d) for s, d in outs], in_specs...  8.88 us
    ppermute x1, waiting for transfers between devices, step(): back_right = lax.ppermute(to_left, DOM, down)  7.14 us
    ppermute x1, starting transfers between devices, step(): from_left = lax.ppermute(own, DOM, up)  6.52 us
    all_gather x1, blocking collectives, step(): sums = lax.all_gather(half, 'c', axis=0, tiled=True)  4.79 us
    all_to_all x2, waiting for transfers between devices, swap(): return lax.all_to_all(x, axes, split_axis=0, concat_axis=0, tiled=True)  4.76 us
    ppermute x1, starting transfers between devices, step(): back_left = lax.ppermute(to_right, DOM, up)  3.9 us
  transfers between devices with their start and end apart: 6, of which 4 were waited for; matrix products, arithmetic and copies ran while one was open for 0% of the time, Pallas kernels for 2%

profile of v4, /device:TPU:63, one launch (start us, length us, event | category | flops | bytes accessed | tf_op | source)
XLA Modules:
  0.0 110.8 jit_solution(6253756413246727127)
XLA Ops:
  0.6 0.0 copy-start.1
  0.6 0.0 copy-start
  0.7 3.1 %collective-permute-start.1 = (bf16[128,256]{1,0:T(8,128)(2,1)}, bf16[128,256]{1,0:T(8,128)(2,1)S(1)}, u32[]{:S(2)}, u32[]{:S(2)}) collective-permute-start(bf16[128,256]{1,0:T(8,128)(2,1)} %bitcast.11), channel_id=1, source_target_pairs={{8,0},{16,8},{24,16},{32,24},{40,32},{48,40},{56,48},{64,56},{72,6... | collective-permute-start | bytes 196616 | tf_op jit(solution)/shard_map/ppermute | solution.py:282
  3.8 6.5 %collective-permute-start = (bf16[128,256]{1,0:T(8,128)(2,1)}, bf16[128,256]{1,0:T(8,128)(2,1)S(1)}, u32[]{:S(2)}, u32[]{:S(2)}) collective-permute-start(bf16[128,256]{1,0:T(8,128)(2,1)} %bitcast.12), channel_id=1, source_target_pairs={{0,8},{8,16},{16,24},{24,32},{32,40},{40,48},{48,56},{56,64},{64,7... | collective-permute-start | bytes 196616 | tf_op jit(solution)/shard_map/ppermute | solution.py:281
  10.3 1.3 %slots.1 = (bf16[2048,384]{1,0:T(8,128)(2,1)S(1)}, f32[128,16]{1,0:T(8,128)S(1)}, s32[16,128]{1,0:T(8,128)S(1)}, bf16[128,256]{1,0:T(8,128)(2,1)S(1)}, bf16[128,...) custom-call(s32[1]{0:T(128)} %bitcast.place, s32[16,128]{1,0:T(8,128)} %bitcast.15, ...), custom_call_target="tpu_custom_call" | custom-call | tf_op jit(solution)/shard_map/slots/pallas_call | solution.py:289
  11.6 0.0 collective-permute-done.1.right
  11.6 0.3 collective-permute-done.left
  11.9 2.0 %shard_map.119 = (bf16[128,256]{1,0:T(8,128)(2,1)S(1)}, bf16[8,2,16,256]{3,2,1,0:T(8,128)(2,1)S(1)}, bf16[2048,256]{1,0:T(8,128)(2,1)S(1)}) custom-call(bf16[128,256]{1,0:T(8,128)(2,1)S(1)} %collective-permute-done.left, bf16[128,256]{1,0:T(8,128)(2,1)S(1)} %get-tuple-element.30.own, bf16[128,256]{1,0:T(8,128)(2,1)S(1)} %collective-permute-done.1.right, ...), custom_call_target="tpu_custom_call" | custom-call | tf_op jit(solution)/shard_map/pallas_call | solution.py:38
  13.9 20.3 %all_to_all.25.got = bf16[8,2,16,256]{3,2,1,0:T(8,128)(2,1)S(1)} all-to-all(bf16[8,2,16,256]{3,2,1,0:T(8,128)(2,1)S(1)} %get-tuple-element.36), channel_id=1, replica_groups=mesh['zl'=2,'x'=4,'yh'=4,'yl'=2,'zh'=4,'c'=2] {'zh','c'}, dimensions={0} | all-to-all | bytes 262144 | tf_op jit(solution)/shard_map/all_to_all | solution.py:271
  34.2 0.0 copy-done.1
  34.2 0.0 copy-done
  34.2 2.0 %shard_map.120 = (bf16[8,16,256]{2,1,0:T(8,128)(2,1)}, bf16[128,256]{1,0:T(8,128)(2,1)S(1)}, bf16[3,128,256]{2,1,0:T(8,128)(2,1)S(1)}) custom-call(bf16[8,2,16,256]{3,2,1,0:T(8,128)(2,1)S(1)} %all_to_all.25.got, bf16[256,768]{1,0:T(8,128)(2,1)S(1)} %copy-done, bf16[256,256]{1,0:T(8,128)(2,1)S(1)} %copy-done.1), custom_call_target="tpu_custom_call" | custom-call | tf_op jit(solution)/shard_map/pallas_call | solution.py:38
  36.2 4.1 %all-to-all-start.1 = ((bf16[8,16,256]{2,1,0:T(8,128)(2,1)}), bf16[8,16,256]{2,1,0:T(8,128)(2,1)S(1)}, u32[]{:S(2)}, u32[]{:S(2)}) async-start(bf16[8,16,256]{2,1,0:T(8,128)(2,1)} %get-tuple-element.37), calls=%async_computation.1 | async-start | bytes 131072 | tf_op jit(solution)/shard_map/all_to_all | solution.py:271
  40.3 0.3 shard_map.123
  40.6 2.2 %all_gather.9.early_both = bf16[2,1024,128]{2,1,0:T(8,128)(2,1)S(1)} all-gather(bf16[1,1024,128]{2,1,0:T(8,128)(2,1)S(1)} %get-tuple-element.48), channel_id=1, replica_groups=mesh['zl'=2,'x'=4,'yh'=4,'yl'=2,'zh'=4,'c'=2] {'c'}, dimensions={0}, use_global_device_ids=true | all-gather | bytes 786432 | tf_op jit(solution)/shard_map/all_gather | solution.py:330
  42.8 4.8 %all-to-all-done.1 = bf16[8,16,256]{2,1,0:T(8,128)(2,1)S(1)} async-done(((bf16[8,16,256]{2,1,0:T(8,128)(2,1)}), bf16[8,16,256]{2,1,0:T(8,128)(2,1)S(1)}, u32[]{:S(2)}, u32[]{:S(2)}) %all-to-all-start.1) | async-done | bytes 65568 | tf_op jit(solution)/shard_map/all_to_all | solution.py:271
  47.6 1.6 %shard_map.121 = (bf16[128,256]{1,0:T(8,128)(2,1)S(1)}, bf16[128,256]{1,0:T(8,128)(2,1)S(1)}, f32[128,256]{1,0:T(8,128)S(1)}, f32[128,256]{1,0:T(8,128)S(1)}, bf...) custom-call(s32[1]{0:T(128)} %bitcast.place, bf16[128,256]{1,0:T(8,128)(2,1)S(1)} %bitcast.8, ...), custom_call_target="tpu_custom_call" | custom-call | tf_op jit(solution)/shard_map/pallas_call | solution.py:38
  49.2 2.6 %all_gather.10.late_both = bf16[2,512,128]{2,1,0:T(8,128)(2,1)S(1)} all-gather(bf16[1,512,128]{2,1,0:T(8,128)(2,1)S(1)} %get-tuple-element.50), channel_id=1, replica_groups=mesh['zl'=2,'x'=4,'yh'=4,'yl'=2,'zh'=4,'c'=2] {'c'}, dimensions={0}, use_global_device_ids=true | all-gather | bytes 393216 | tf_op jit(solution)/shard_map/all_gather | solution.py:353
  51.7 0.1 shard_map.124
  51.9 10.5 %all_to_all.26.parts = bf16[16,96,128]{2,1,0:T(8,128)(2,1)S(1)} all-to-all(bf16[16,96,128]{2,1,0:T(8,128)(2,1)S(1)} %shard_map.124), channel_id=1, replica_groups=mesh['zl'=2,'x'=4,'yh'=4,'yl'=2,'zh'=4,'c'=2] {'zl','x','yl'}, dimensions={0} | all-to-all | bytes 786432 | tf_op jit(solution)/shard_map/all_to_all | solution.py:271
  62.4 0.1 shard_map.125
  62.4 19.3 %all_to_all.27.parts = bf16[16,96,128]{2,1,0:T(8,128)(2,1)S(1)} all-to-all(bf16[16,96,128]{2,1,0:T(8,128)(2,1)S(1)} %shard_map.125), channel_id=1, replica_groups=mesh['zl'=2,'x'=4,'yh'=4,'yl'=2,'zh'=4,'c'=2] {'yh','zh'}, dimensions={0} | all-to-all | bytes 786432 | tf_op jit(solution)/shard_map/all_to_all | solution.py:271
  81.7 0.8 shard_map.126
  82.5 8.4 %all-to-all-start.4 = ((bf16[16,96,128]{2,1,0:T(8,128)(2,1)}), bf16[16,96,128]{2,1,0:T(8,128)(2,1)S(1)}, u32[]{:S(2)}, u32[]{:S(2)}) async-start(bf16[16,96,128]{2,1,0:T(8,128)(2,1)} %shard_map.126), calls=%async_computation.4 | async-start | bytes 786432 | tf_op jit(solution)/shard_map/all_to_all | solution.py:271
  90.9 3.9 %collective-permute-start.2 = (bf16[128,256]{1,0:T(8,128)(2,1)S(1)}, bf16[128,256]{1,0:T(8,128)(2,1)S(1)}, u32[]{:S(2)}, u32[]{:S(2)}) collective-permute-start(bf16[128,256]{1,0:T(8,128)(2,1)S(1)} %get-tuple-element.43), channel_id=1, source_target_pairs={{0,8},{8,16},{16,24},{24,32},{32,40},{40,48},{48,56},{56,64},{64,7... | collective-permute-start | bytes 196616 | tf_op jit(solution)/shard_map/ppermute | solution.py:345
  94.8 1.9 %collective-permute-start.3 = (bf16[128,256]{1,0:T(8,128)(2,1)S(1)}, bf16[128,256]{1,0:T(8,128)(2,1)S(1)}, u32[]{:S(2)}, u32[]{:S(2)}) collective-permute-start(bf16[128,256]{1,0:T(8,128)(2,1)S(1)} %get-tuple-element.44), channel_id=1, source_target_pairs={{8,0},{16,8},{24,16},{32,24},{40,32},{48,40},{56,48},{64,56},{72,6... | collective-permute-start | bytes 196616 | tf_op jit(solution)/shard_map/ppermute | solution.py:346
  96.7 0.2 collective-permute-done.2.from_left
  96.9 7.1 %collective-permute-done.3.from_right = bf16[128,256]{1,0:T(8,128)(2,1)S(1)} collective-permute-done((bf16[128,256]{1,0:T(8,128)(2,1)S(1)}, bf16[128,256]{1,0:T(8,128)(2,1)S(1)}, u32[]{:S(2)}, u32[]{:S(2)}) %collective-permute-start.3) | collective-permute-done | bytes 65568 | tf_op jit(solution)/shard_map/ppermute | solution.py:346
  104.0 0.8 shard_map.122
  104.9 0.0 all-to-all-done.4
  104.9 4.8 %all_gather.11.refs_0_ = bf16[2,1536,128]{2,1,0:T(8,128)(2,1)S(1)} all-gather(bf16[1,1536,128]{2,1,0:T(8,128)(2,1)S(1)} %bitcast.9), channel_id=1, replica_groups=mesh['zl'=2,'x'=4,'yh'=4,'yl'=2,'zh'=4,'c'=2] {'c'}, dimensions={0}, use_global_device_ids=true | all-gather | bytes 1179648 | tf_op jit(solution)/shard_map/all_gather | solution.py:368
  109.7 1.2 %shard_map.127 = (f32[256,256]{1,0:T(8,128)}, f32[256,256]{1,0:T(8,128)}, f32[256,768]{1,0:T(8,128)}, f32[256,256]{1,0:T(8,128)}) custom-call(bf16[2,1536,128]{2,1,0:T(8,128)(2,1)S(1)} %all_gather.11.refs_0_), custom_call_target="tpu_custom_call" | custom-call | tf_op jit(solution)/shard_map/pallas_call | solution.py:38
Async XLA Ops:
  0.6 33.5 %copy-start.1 = (bf16[256,256]{1,0:T(8,128)(2,1)S(1)}, bf16[256,256]{1,0:T(8,128)(2,1)}, u32[]{:S(2)}) copy-start(bf16[256,256]{1,0:T(8,128)(2,1)} %oproj.1) | copy-start | bytes 393220
  0.6 33.5 %copy-start = (bf16[256,768]{1,0:T(8,128)(2,1)S(1)}, bf16[256,768]{1,0:T(8,128)(2,1)}, u32[]{:S(2)}) copy-start(bf16[256,768]{1,0:T(8,128)(2,1)} %aproj.1) | copy-start | bytes 1179652
  0.7 10.9 %collective-permute-start.1 = (bf16[128,256]{1,0:T(8,128)(2,1)}, bf16[128,256]{1,0:T(8,128)(2,1)S(1)}, u32[]{:S(2)}, u32[]{:S(2)}) collective-permute-start(bf16[128,256]{1,0:T(8,128)(2,1)} %bitcast.11), channel_id=1, source_target_pairs={{8,0},{16,8},{24,16},{32,24},{40,32},{48,40},{56,48},{64,56},{72,6... | collective-permute-start | bytes 196616 | tf_op jit(solution)/shard_map/ppermute | solution.py:282
  3.8 8.2 %collective-permute-start = (bf16[128,256]{1,0:T(8,128)(2,1)}, bf16[128,256]{1,0:T(8,128)(2,1)S(1)}, u32[]{:S(2)}, u32[]{:S(2)}) collective-permute-start(bf16[128,256]{1,0:T(8,128)(2,1)} %bitcast.12), channel_id=1, source_target_pairs={{0,8},{8,16},{16,24},{24,32},{32,40},{40,48},{48,56},{56,64},{64,7... | collective-permute-start | bytes 196616 | tf_op jit(solution)/shard_map/ppermute | solution.py:281
  36.2 11.4 %all-to-all-start.1 = ((bf16[8,16,256]{2,1,0:T(8,128)(2,1)}), bf16[8,16,256]{2,1,0:T(8,128)(2,1)S(1)}, u32[]{:S(2)}, u32[]{:S(2)}) async-start(bf16[8,16,256]{2,1,0:T(8,128)(2,1)} %get-tuple-element.37), calls=%async_computation.1 | async-start | bytes 131072 | tf_op jit(solution)/shard_map/all_to_all | solution.py:271
  82.5 22.4 %all-to-all-start.4 = ((bf16[16,96,128]{2,1,0:T(8,128)(2,1)}), bf16[16,96,128]{2,1,0:T(8,128)(2,1)S(1)}, u32[]{:S(2)}, u32[]{:S(2)}) async-start(bf16[16,96,128]{2,1,0:T(8,128)(2,1)} %shard_map.126), calls=%async_computation.4 | async-start | bytes 786432 | tf_op jit(solution)/shard_map/all_to_all | solution.py:271
  90.9 6.0 %collective-permute-start.2 = (bf16[128,256]{1,0:T(8,128)(2,1)S(1)}, bf16[128,256]{1,0:T(8,128)(2,1)S(1)}, u32[]{:S(2)}, u32[]{:S(2)}) collective-permute-start(bf16[128,256]{1,0:T(8,128)(2,1)S(1)} %get-tuple-element.43), channel_id=1, source_target_pairs={{0,8},{8,16},{16,24},{24,32},{32,40},{40,48},{48,56},{56,64},{64,7... | collective-permute-start | bytes 196616 | tf_op jit(solution)/shard_map/ppermute | solution.py:345
  94.8 9.2 %collective-permute-start.3 = (bf16[128,256]{1,0:T(8,128)(2,1)S(1)}, bf16[128,256]{1,0:T(8,128)(2,1)S(1)}, u32[]{:S(2)}, u32[]{:S(2)}) collective-permute-start(bf16[128,256]{1,0:T(8,128)(2,1)S(1)} %get-tuple-element.44), channel_id=1, source_target_pairs={{8,0},{16,8},{24,16},{32,24},{40,32},{48,40},{56,48},{64,56},{72,6... | collective-permute-start | bytes 196616 | tf_op jit(solution)/shard_map/ppermute | solution.py:346

commit v5 on v4

--- a/solution.py
+++ b/solution.py
@@ -30,7 +30,7 @@
 SMEM = pl.BlockSpec(memory_space=pltpu.SMEM)
 
 
-def call(kernel, outs, args, scratch=(), scalars=0, stored=False):
+def call(kernel, outs, args, scratch=(), scalars=0, stored=False, own_copies=False):
     bound = []
     for n, a in enumerate(args):
         bound.append(a if n < scalars else pltpu.with_memory_space_constraint(a, pltpu.VMEM))
@@ -39,7 +39,7 @@
         kernel,
         out_shape=[place(s, d) for s, d in outs],
         in_specs=[SMEM if n < scalars else VMEM for n in range(len(args))],
-        out_specs=[VMEM] * len(outs),
+        out_specs=[pl.BlockSpec(memory_space=pl.ANY) if own_copies else VMEM] * len(outs),
         scratch_shapes=list(scratch),
         compiler_params=pltpu.CompilerParams(vmem_limit_bytes=24 * 2**20),
     )(*bound)
@@ -85,32 +85,39 @@
         hot[k * rows : (k + 1) * rows] = jnp.where(mark, 1.0, 0.0).astype(bf16)
     degree = table[:, slots : slots + 1]
     slot = lax.broadcasted_iota(jnp.int32, (rows, slots), 1).astype(f32)
-    weights[...] = jnp.where(slot < degree, 1.0 / degree, 0.0)
+    weights[...] = jnp.where(slot < degree, 0.5 / degree, 0.0)
     for copy in copies[2:]:
         copy.wait()
 
 
-def forward_kernel(left, own, right, cot, hot, weights, mproj, cproj, combined, sent, slopew, ext):
+def forward_kernel(left, own, right, cot, hot, weights, mproj, cproj, combined, sent, slopew, ext, picked):
     ext[:HALO] = left[...]
     ext[HALO : HALO + 128] = own[...]
     ext[HALO + 128 :] = right[...]
     rows = own.shape[0]
     own_f = own[...].astype(f32)
+    half_own = 0.5 * own_f
+    half_proj = (0.5 * mproj[...].astype(f32)).astype(bf16)
     total = jnp.zeros((rows, WIDTH), f32)
     group = 4
+    span = group * rows
+
+    def pick(g):
+        picked[g * span : (g + 1) * span] = mm(hot[g * span : (g + 1) * span], ext[...]).astype(bf16)
+
+    pick(0)
     for g in range(SLOTS // group):
-        span = group * rows
-        picked = mm(hot[g * span : (g + 1) * span], ext[...]).astype(bf16)
-        message = mm(picked, mproj[...])
+        if g + 1 < SLOTS // group:
+            pick(g + 1)
         for j in range(group):
             k = g * group + j
-            weight = weights[:, k : k + 1]
-            before = message[j * rows : (j + 1) * rows] + own_f
-            logistic = 0.5 * jnp.tanh(0.5 * before) + 0.5
-            value = before * logistic
-            total = total + value * weight
-            slope = logistic + logistic * (before - value)
-            slopew[k * rows : (k + 1) * rows] = (slope * weight).astype(bf16)
+            one = slice(k * rows, (k + 1) * rows)
+            u = mm(picked[one], half_proj) + half_own
+            t = jnp.tanh(u)
+            share = (1.0 + t) * weights[:, k : k + 1]
+            total = total + u * share
+            slopew[one] = (share * (1.0 + u * (1.0 - t))).astype(bf16)
+    total = total + total
     comb = total.astype(bf16)
     combined[...] = comb
     spatial = (own_f + mm(comb, cproj[...])).astype(bf16)
@@ -204,10 +211,17 @@
     gs = gs_ref[...]
     gc = mm_nt(gs, cproj[...])
     total = gs.astype(f32)
-    below = lax.broadcasted_iota(jnp.int32, (3 * HALO, rows), 0)
+    below = lax.broadcasted_iota(jnp.int32, (HALO, rows), 0).astype(f32).astype(bf16)
+    one = jnp.ones((HALO, rows), bf16)
+    nbr = nbrt[...]
+    for part in range(3):
+        near = nbr - part * HALO
+        near = jnp.where((near >= 0) & (near < HALO), near, -1).astype(f32).astype(bf16)
+        for k in range(SLOTS):
+            mark = near[k : k + 1, :] == below
+            hot[part * HALO : (part + 1) * HALO, k * rows : (k + 1) * rows] = jnp.where(mark, one, 0 * one)
     for k in range(SLOTS):
         span = slice(k * rows, (k + 1) * rows)
-        hot[:, span] = jnp.where(nbrt[k : k + 1, :] == below, 1.0, 0.0).astype(bf16)
         grad_before = gc * slopew[span].astype(f32)
         total = total + grad_before
         gb[span] = grad_before.astype(bf16)
@@ -248,23 +262,36 @@
         out[p] = total
 
 
-def final_kernel(factor, sums, message, combine, attend, output):
-    def get(half, index):
+def spread_kernel(parts, out, total_ref, sems):
+    total = parts[0].astype(f32)
+    for p in range(1, parts.shape[0]):
+        total = total + parts[p].astype(f32)
+    total_ref[...] = total.astype(bf16)
+    copies = [pltpu.make_async_copy(total_ref, out.at[p], sems.at[p]) for p in range(out.shape[0])]
+    for copy in copies:
+        copy.start()
+    for copy in copies:
+        copy.wait()
+
+
+def final_kernel(factor, sums, message, combine, attend, output, blocks, sems):
+    places = (
+        (attend.at[:, :WIDTH], 0, 0),
+        (attend.at[:, WIDTH : 2 * WIDTH], 0, 1),
+        (attend.at[:, 2 * WIDTH :], 1, 0),
+        (output, 1, 1),
+        (message, 0, 2),
+        (combine, 1, 2),
+    )
+    copies = []
+    for n, (target, half, index) in enumerate(places):
         base = index * 2 * WIDTH
-        first = sums[half, base : base + WIDTH, :].astype(f32) * factor
-        second = sums[half, base + WIDTH : base + 2 * WIDTH, :].astype(f32) * factor
-        return first, second
-
-    def put(ref, at, pair):
-        ref[:, at : at + LANES] = pair[0]
-        ref[:, at + LANES : at + 2 * LANES] = pair[1]
-
-    put(attend, 0, get(0, 0))
-    put(attend, WIDTH, get(0, 1))
-    put(attend, 2 * WIDTH, get(1, 0))
-    put(output, 0, get(1, 1))
-    put(message, 0, get(0, 2))
-    put(combine, 0, get(1, 2))
+        blocks[n, :, :LANES] = sums[half, base : base + WIDTH, :].astype(f32) * factor
+        blocks[n, :, LANES:] = sums[half, base + WIDTH : base + 2 * WIDTH, :].astype(f32) * factor
+        copies.append(pltpu.make_async_copy(blocks.at[n], target, sems.at[n]))
+        copies[-1].start()
+    for copy in copies:
+        copy.wait()
 
 
 def swap(x, axes):
@@ -311,7 +338,10 @@
         forward_kernel,
         [((rows, width), bf16), ((SNAPS, 2, rows // SNAPS, width), bf16), ((edges, width), bf16)],
         (from_left, own, from_right, cot, hot, weights, mproj, cproj),
-        [pltpu.VMEM((3 * HALO, width), bf16)],
+        [
+            pltpu.VMEM((3 * HALO, width), bf16),
+            pltpu.VMEM((edges, width), bf16),
+        ],
     )
     got = swap(sent, SNAP)
     grads, att, three = call(
@@ -345,23 +375,22 @@
     back_left = lax.ppermute(to_right, DOM, up)
     back_right = lax.ppermute(to_left, DOM, down)
     (grad_features,) = call(
-        features_kernel,
-        [((rows, width), bf16)],
-        (base, own_rows, back_left, back_right, mproj),
-        stored=True,
+        features_kernel, [((rows, width), bf16)], (base, own_rows, back_left, back_right, mproj), stored=True
     )
     late_both = lax.all_gather(send, "c", axis=0, tiled=True)
     count = lax.axis_size(SCATTER)
     across = lax.axis_size(ACROSS)
     piece = 6 * width // count
-    (mine,) = call(
-        pair_kernel,
-        [((count, piece, LANES), bf16)],
-        (where, early, early_both, keep, late_both),
-        scalars=1,
-    )
+    (mine,) = call(pair_kernel, [((count, piece, LANES), bf16)], (where, early, early_both, keep, late_both), scalars=1)
     parts = swap(mine, SCATTER)
-    (spread,) = call(fold_kernel, [((across, piece, LANES), bf16)], (parts,))
+    (spread,) = call(
+        spread_kernel,
+        [((across, piece, LANES), bf16)],
+        (parts,),
+        [pltpu.VMEM((piece, LANES), bf16), pltpu.SemaphoreType.DMA((across,))],
+        stored=True,
+        own_copies=True,
+    )
     parts = swap(spread, ACROSS)
     (whole,) = call(fold_kernel, [((count, piece, LANES), bf16)], (parts,))
     half = swap(whole, SCATTER).reshape(1, 6 * width, LANES)
@@ -375,7 +404,9 @@
         last,
         [((width, width), f32), ((width, width), f32), ((width, 3 * width), f32), ((width, width), f32)],
         (sums,),
+        [pltpu.VMEM((6, width, width), f32), pltpu.SemaphoreType.DMA((6,))],
         stored=True,
+        own_copies=True,
     )
     return grad_features[None], message, combine, attend, output
 

time: 111 us -> 111 us (level)
  no operation moved by 1% of the time
where the time goes in v5:
time: 111 us
  blocking collectives  59.6 us (54%)
  starting transfers between devices  28 us (25%)
  waiting for transfers between devices  12.4 us (11%)
  Pallas kernels  10.2 us (9%)
    all_to_all x3, blocking collectives, swap(): return lax.all_to_all(x, axes, split_axis=0, concat_axis=0, tiled=True)  50 us
    all_to_all x2, starting transfers between devices, swap(): return lax.all_to_all(x, axes, split_axis=0, concat_axis=0, tiled=True)  12.5 us
    pallas_call x9, Pallas kernels, call(): pl.pallas_call(kernel, out_shape=[place(s, d) for s, d in outs], in_specs...  8.92 us
    ppermute x1, waiting for transfers between devices, step(): back_right = lax.ppermute(to_left, DOM, down)  7.14 us
    ppermute x1, starting transfers between devices, step(): from_left = lax.ppermute(own, DOM, up)  6.52 us
    all_gather x1, blocking collectives, step(): sums = lax.all_gather(half, 'c', axis=0, tiled=True)  4.78 us
    all_to_all x2, waiting for transfers between devices, swap(): return lax.all_to_all(x, axes, split_axis=0, concat_axis=0, tiled=True)  4.76 us
    ppermute x1, starting transfers between devices, step(): back_left = lax.ppermute(to_right, DOM, up)  3.9 us
  transfers between devices with their start and end apart: 6, of which 4 were waited for; matrix products, arithmetic and copies ran while one was open for 0% of the time, Pallas kernels for 2%

profile of v5, /device:TPU:63, one launch (start us, length us, event | category | flops | bytes accessed | tf_op | source)
XLA Modules:
  0.0 110.9 jit_solution(7015133896306289102)
XLA Ops:
  0.6 0.0 copy-start.1
  0.6 0.0 copy-start
  0.7 3.1 %collective-permute-start.1 = (bf16[128,256]{1,0:T(8,128)(2,1)}, bf16[128,256]{1,0:T(8,128)(2,1)S(1)}, u32[]{:S(2)}, u32[]{:S(2)}) collective-permute-start(bf16[128,256]{1,0:T(8,128)(2,1)} %bitcast.11), channel_id=1, source_target_pairs={{8,0},{16,8},{24,16},{32,24},{40,32},{48,40},{56,48},{64,56},{72,6... | collective-permute-start | bytes 196616 | tf_op jit(solution)/shard_map/ppermute | solution.py:309
  3.8 6.5 %collective-permute-start = (bf16[128,256]{1,0:T(8,128)(2,1)}, bf16[128,256]{1,0:T(8,128)(2,1)S(1)}, u32[]{:S(2)}, u32[]{:S(2)}) collective-permute-start(bf16[128,256]{1,0:T(8,128)(2,1)} %bitcast.12), channel_id=1, source_target_pairs={{0,8},{8,16},{16,24},{24,32},{32,40},{40,48},{48,56},{56,64},{64,7... | collective-permute-start | bytes 196616 | tf_op jit(solution)/shard_map/ppermute | solution.py:308
  10.3 1.3 %slots.1 = (bf16[2048,384]{1,0:T(8,128)(2,1)S(1)}, f32[128,16]{1,0:T(8,128)S(1)}, s32[16,128]{1,0:T(8,128)S(1)}, bf16[128,256]{1,0:T(8,128)(2,1)S(1)}, bf16[128,...) custom-call(s32[1]{0:T(128)} %bitcast.place, s32[16,128]{1,0:T(8,128)} %bitcast.15, ...), custom_call_target="tpu_custom_call" | custom-call | tf_op jit(solution)/shard_map/slots/pallas_call | solution.py:316
  11.6 0.0 collective-permute-done.1.right
  11.6 0.3 collective-permute-done.left
  11.9 1.4 %shard_map.119 = (bf16[128,256]{1,0:T(8,128)(2,1)S(1)}, bf16[8,2,16,256]{3,2,1,0:T(8,128)(2,1)S(1)}, bf16[2048,256]{1,0:T(8,128)(2,1)S(1)}) custom-call(bf16[128,256]{1,0:T(8,128)(2,1)S(1)} %collective-permute-done.left, bf16[128,256]{1,0:T(8,128)(2,1)S(1)} %get-tuple-element.30.own, bf16[128,256]{1,0:T(8,128)(2,1)S(1)} %collective-permute-done.1.right, ...), custom_call_target="tpu_custom_call" | custom-call | tf_op jit(solution)/shard_map/pallas_call | solution.py:38
  13.3 20.2 %all_to_all.25.got = bf16[8,2,16,256]{3,2,1,0:T(8,128)(2,1)S(1)} all-to-all(bf16[8,2,16,256]{3,2,1,0:T(8,128)(2,1)S(1)} %get-tuple-element.36), channel_id=1, replica_groups=mesh['zl'=2,'x'=4,'yh'=4,'yl'=2,'zh'=4,'c'=2] {'zh','c'}, dimensions={0} | all-to-all | bytes 262144 | tf_op jit(solution)/shard_map/all_to_all | solution.py:298
  33.6 0.0 copy-done.1
  33.6 0.0 copy-done
  33.6 2.0 %shard_map.120 = (bf16[8,16,256]{2,1,0:T(8,128)(2,1)}, bf16[128,256]{1,0:T(8,128)(2,1)S(1)}, bf16[3,128,256]{2,1,0:T(8,128)(2,1)S(1)}) custom-call(bf16[8,2,16,256]{3,2,1,0:T(8,128)(2,1)S(1)} %all_to_all.25.got, bf16[256,768]{1,0:T(8,128)(2,1)S(1)} %copy-done, bf16[256,256]{1,0:T(8,128)(2,1)S(1)} %copy-done.1), custom_call_target="tpu_custom_call" | custom-call | tf_op jit(solution)/shard_map/pallas_call | solution.py:38
  35.6 4.1 %all-to-all-start.1 = ((bf16[8,16,256]{2,1,0:T(8,128)(2,1)}), bf16[8,16,256]{2,1,0:T(8,128)(2,1)S(1)}, u32[]{:S(2)}, u32[]{:S(2)}) async-start(bf16[8,16,256]{2,1,0:T(8,128)(2,1)} %get-tuple-element.37), calls=%async_computation.1 | async-start | bytes 131072 | tf_op jit(solution)/shard_map/all_to_all | solution.py:298
  39.7 0.3 shard_map.123
  40.1 2.2 %all_gather.9.early_both = bf16[2,1024,128]{2,1,0:T(8,128)(2,1)S(1)} all-gather(bf16[1,1024,128]{2,1,0:T(8,128)(2,1)S(1)} %get-tuple-element.48), channel_id=1, replica_groups=mesh['zl'=2,'x'=4,'yh'=4,'yl'=2,'zh'=4,'c'=2] {'c'}, dimensions={0}, use_global_device_ids=true | all-gather | bytes 786432 | tf_op jit(solution)/shard_map/all_gather | solution.py:360
  42.2 4.8 %all-to-all-done.1 = bf16[8,16,256]{2,1,0:T(8,128)(2,1)S(1)} async-done(((bf16[8,16,256]{2,1,0:T(8,128)(2,1)}), bf16[8,16,256]{2,1,0:T(8,128)(2,1)S(1)}, u32[]{:S(2)}, u32[]{:S(2)}) %all-to-all-start.1) | async-done | bytes 65568 | tf_op jit(solution)/shard_map/all_to_all | solution.py:298
  47.0 1.5 %shard_map.121 = (bf16[128,256]{1,0:T(8,128)(2,1)S(1)}, bf16[128,256]{1,0:T(8,128)(2,1)S(1)}, f32[128,256]{1,0:T(8,128)S(1)}, f32[128,256]{1,0:T(8,128)S(1)}, bf...) custom-call(s32[1]{0:T(128)} %bitcast.place, bf16[128,256]{1,0:T(8,128)(2,1)S(1)} %bitcast.8, ...), custom_call_target="tpu_custom_call" | custom-call | tf_op jit(solution)/shard_map/pallas_call | solution.py:38
  48.5 2.6 %all_gather.10.late_both = bf16[2,512,128]{2,1,0:T(8,128)(2,1)S(1)} all-gather(bf16[1,512,128]{2,1,0:T(8,128)(2,1)S(1)} %get-tuple-element.50), channel_id=1, replica_groups=mesh['zl'=2,'x'=4,'yh'=4,'yl'=2,'zh'=4,'c'=2] {'c'}, dimensions={0}, use_global_device_ids=true | all-gather | bytes 393216 | tf_op jit(solution)/shard_map/all_gather | solution.py:380
  51.1 0.1 shard_map.124
  51.2 10.5 %all_to_all.26.parts = bf16[16,96,128]{2,1,0:T(8,128)(2,1)S(1)} all-to-all(bf16[16,96,128]{2,1,0:T(8,128)(2,1)S(1)} %shard_map.124), channel_id=1, replica_groups=mesh['zl'=2,'x'=4,'yh'=4,'yl'=2,'zh'=4,'c'=2] {'zl','x','yl'}, dimensions={0} | all-to-all | bytes 786432 | tf_op jit(solution)/shard_map/all_to_all | solution.py:298
  61.7 0.7 shard_map.125
  62.4 19.3 %all_to_all.27.parts = bf16[16,96,128]{2,1,0:T(8,128)(2,1)S(1)} all-to-all(bf16[16,96,128]{2,1,0:T(8,128)(2,1)S(1)} %shard_map.125), channel_id=1, replica_groups=mesh['zl'=2,'x'=4,'yh'=4,'yl'=2,'zh'=4,'c'=2] {'yh','zh'}, dimensions={0} | all-to-all | bytes 786432 | tf_op jit(solution)/shard_map/all_to_all | solution.py:298
  81.7 0.8 shard_map.126
  82.5 8.4 %all-to-all-start.4 = ((bf16[16,96,128]{2,1,0:T(8,128)(2,1)}), bf16[16,96,128]{2,1,0:T(8,128)(2,1)S(1)}, u32[]{:S(2)}, u32[]{:S(2)}) async-start(bf16[16,96,128]{2,1,0:T(8,128)(2,1)} %shard_map.126), calls=%async_computation.4 | async-start | bytes 786432 | tf_op jit(solution)/shard_map/all_to_all | solution.py:298
  90.9 3.9 %collective-permute-start.2 = (bf16[128,256]{1,0:T(8,128)(2,1)S(1)}, bf16[128,256]{1,0:T(8,128)(2,1)S(1)}, u32[]{:S(2)}, u32[]{:S(2)}) collective-permute-start(bf16[128,256]{1,0:T(8,128)(2,1)S(1)} %get-tuple-element.43), channel_id=1, source_target_pairs={{0,8},{8,16},{16,24},{24,32},{32,40},{40,48},{48,56},{56,64},{64,7... | collective-permute-start | bytes 196616 | tf_op jit(solution)/shard_map/ppermute | solution.py:375
  94.8 1.9 %collective-permute-start.3 = (bf16[128,256]{1,0:T(8,128)(2,1)S(1)}, bf16[128,256]{1,0:T(8,128)(2,1)S(1)}, u32[]{:S(2)}, u32[]{:S(2)}) collective-permute-start(bf16[128,256]{1,0:T(8,128)(2,1)S(1)} %get-tuple-element.44), channel_id=1, source_target_pairs={{8,0},{16,8},{24,16},{32,24},{40,32},{48,40},{56,48},{64,56},{72,6... | collective-permute-start | bytes 196616 | tf_op jit(solution)/shard_map/ppermute | solution.py:376
  96.7 0.2 collective-permute-done.2.from_left
  96.9 7.1 %collective-permute-done.3.from_right = bf16[128,256]{1,0:T(8,128)(2,1)S(1)} collective-permute-done((bf16[128,256]{1,0:T(8,128)(2,1)S(1)}, bf16[128,256]{1,0:T(8,128)(2,1)S(1)}, u32[]{:S(2)}, u32[]{:S(2)}) %collective-permute-start.3) | collective-permute-done | bytes 65568 | tf_op jit(solution)/shard_map/ppermute | solution.py:376
  104.0 0.8 shard_map.122
  104.9 0.0 all-to-all-done.4
  104.9 4.8 %all_gather.11.refs_0_ = bf16[2,1536,128]{2,1,0:T(8,128)(2,1)S(1)} all-gather(bf16[1,1536,128]{2,1,0:T(8,128)(2,1)S(1)} %bitcast.9), channel_id=1, replica_groups=mesh['zl'=2,'x'=4,'yh'=4,'yl'=2,'zh'=4,'c'=2] {'c'}, dimensions={0}, use_global_device_ids=true | all-gather | bytes 1179648 | tf_op jit(solution)/shard_map/all_gather | solution.py:397
  109.7 1.2 %shard_map.127 = (f32[256,256]{1,0:T(8,128)}, f32[256,256]{1,0:T(8,128)}, f32[256,768]{1,0:T(8,128)}, f32[256,256]{1,0:T(8,128)}) custom-call(bf16[2,1536,128]{2,1,0:T(8,128)(2,1)S(1)} %all_gather.11.refs_0_), custom_call_target="tpu_custom_call" | custom-call | tf_op jit(solution)/shard_map/pallas_call | solution.py:38
Async XLA Ops:
  0.6 32.9 %copy-start.1 = (bf16[256,256]{1,0:T(8,128)(2,1)S(1)}, bf16[256,256]{1,0:T(8,128)(2,1)}, u32[]{:S(2)}) copy-start(bf16[256,256]{1,0:T(8,128)(2,1)} %oproj.1) | copy-start | bytes 393220
  0.6 32.9 %copy-start = (bf16[256,768]{1,0:T(8,128)(2,1)S(1)}, bf16[256,768]{1,0:T(8,128)(2,1)}, u32[]{:S(2)}) copy-start(bf16[256,768]{1,0:T(8,128)(2,1)} %aproj.1) | copy-start | bytes 1179652
  0.7 10.9 %collective-permute-start.1 = (bf16[128,256]{1,0:T(8,128)(2,1)}, bf16[128,256]{1,0:T(8,128)(2,1)S(1)}, u32[]{:S(2)}, u32[]{:S(2)}) collective-permute-start(bf16[128,256]{1,0:T(8,128)(2,1)} %bitcast.11), channel_id=1, source_target_pairs={{8,0},{16,8},{24,16},{32,24},{40,32},{48,40},{56,48},{64,56},{72,6... | collective-permute-start | bytes 196616 | tf_op jit(solution)/shard_map/ppermute | solution.py:309
  3.8 8.2 %collective-permute-start = (bf16[128,256]{1,0:T(8,128)(2,1)}, bf16[128,256]{1,0:T(8,128)(2,1)S(1)}, u32[]{:S(2)}, u32[]{:S(2)}) collective-permute-start(bf16[128,256]{1,0:T(8,128)(2,1)} %bitcast.12), channel_id=1, source_target_pairs={{0,8},{8,16},{16,24},{24,32},{32,40},{40,48},{48,56},{56,64},{64,7... | collective-permute-start | bytes 196616 | tf_op jit(solution)/shard_map/ppermute | solution.py:308
  35.6 11.4 %all-to-all-start.1 = ((bf16[8,16,256]{2,1,0:T(8,128)(2,1)}), bf16[8,16,256]{2,1,0:T(8,128)(2,1)S(1)}, u32[]{:S(2)}, u32[]{:S(2)}) async-start(bf16[8,16,256]{2,1,0:T(8,128)(2,1)} %get-tuple-element.37), calls=%async_computation.1 | async-start | bytes 131072 | tf_op jit(solution)/shard_map/all_to_all | solution.py:298
  82.5 22.4 %all-to-all-start.4 = ((bf16[16,96,128]{2,1,0:T(8,128)(2,1)}), bf16[16,96,128]{2,1,0:T(8,128)(2,1)S(1)}, u32[]{:S(2)}, u32[]{:S(2)}) async-start(bf16[16,96,128]{2,1,0:T(8,128)(2,1)} %shard_map.126), calls=%async_computation.4 | async-start | bytes 786432 | tf_op jit(solution)/shard_map/all_to_all | solution.py:298
  90.9 6.0 %collective-permute-start.2 = (bf16[128,256]{1,0:T(8,128)(2,1)S(1)}, bf16[128,256]{1,0:T(8,128)(2,1)S(1)}, u32[]{:S(2)}, u32[]{:S(2)}) collective-permute-start(bf16[128,256]{1,0:T(8,128)(2,1)S(1)} %get-tuple-element.43), channel_id=1, source_target_pairs={{0,8},{8,16},{16,24},{24,32},{32,40},{40,48},{48,56},{56,64},{64,7... | collective-permute-start | bytes 196616 | tf_op jit(solution)/shard_map/ppermute | solution.py:375
  94.8 9.2 %collective-permute-start.3 = (bf16[128,256]{1,0:T(8,128)(2,1)S(1)}, bf16[128,256]{1,0:T(8,128)(2,1)S(1)}, u32[]{:S(2)}, u32[]{:S(2)}) collective-permute-start(bf16[128,256]{1,0:T(8,128)(2,1)S(1)} %get-tuple-element.44), channel_id=1, source_target_pairs={{8,0},{16,8},{24,16},{32,24},{40,32},{48,40},{56,48},{64,56},{72,6... | collective-permute-start | bytes 196616 | tf_op jit(solution)/shard_map/ppermute | solution.py:376

commit v6 on v5

--- a/solution.py
+++ b/solution.py
@@ -21,7 +21,7 @@
 FINE_NAMES = ("zl", "x", "yh", "yl", "zh", "c")
 DOM = ("zl", "x", "yh", "yl")
 SNAP = ("zh", "c")
-SCATTER = ("zl", "x", "yl")
+SCATTER = ("x", "zl", "yl")
 ACROSS = ("yh", "zh")
 
 f32 = jnp.float32
@@ -260,18 +260,6 @@
     total = total.astype(bf16)
     for p in range(out.shape[0]):
         out[p] = total
-
-
-def spread_kernel(parts, out, total_ref, sems):
-    total = parts[0].astype(f32)
-    for p in range(1, parts.shape[0]):
-        total = total + parts[p].astype(f32)
-    total_ref[...] = total.astype(bf16)
-    copies = [pltpu.make_async_copy(total_ref, out.at[p], sems.at[p]) for p in range(out.shape[0])]
-    for copy in copies:
-        copy.start()
-    for copy in copies:
-        copy.wait()
 
 
 def final_kernel(factor, sums, message, combine, attend, output, blocks, sems):
@@ -383,14 +371,7 @@
     piece = 6 * width // count
     (mine,) = call(pair_kernel, [((count, piece, LANES), bf16)], (where, early, early_both, keep, late_both), scalars=1)
     parts = swap(mine, SCATTER)
-    (spread,) = call(
-        spread_kernel,
-        [((across, piece, LANES), bf16)],
-        (parts,),
-        [pltpu.VMEM((piece, LANES), bf16), pltpu.SemaphoreType.DMA((across,))],
-        stored=True,
-        own_copies=True,
-    )
+    (spread,) = call(fold_kernel, [((across, piece, LANES), bf16)], (parts,))
     parts = swap(spread, ACROSS)
     (whole,) = call(fold_kernel, [((count, piece, LANES), bf16)], (parts,))
     half = swap(whole, SCATTER).reshape(1, 6 * width, LANES)

time: 111 us -> 111 us (level)
  blocking collectives: 59.6 us -> 62.1 us
  starting transfers between devices: 28 us -> 26.2 us
    all_to_all x3, blocking collectives: 50 us -> 52.2 us  [swap(): return lax.all_to_all(x, axes, split_axis=0, concat_axis=0, tiled=True)]
    all_to_all x2, starting transfers between devices: 12.5 us -> 10.9 us  [swap(): return lax.all_to_all(x, axes, split_axis=0, concat_axis=0, tiled=True)]
where the time goes in v6:
time: 111 us
  blocking collectives  62.1 us (56%)
  starting transfers between devices  26.2 us (24%)
  waiting for transfers between devices  12.4 us (11%)
  Pallas kernels  9.52 us (9%)
    all_to_all x3, blocking collectives, swap(): return lax.all_to_all(x, axes, split_axis=0, concat_axis=0, tiled=True)  52.2 us
    all_to_all x2, starting transfers between devices, swap(): return lax.all_to_all(x, axes, split_axis=0, concat_axis=0, tiled=True)  10.9 us
    pallas_call x9, Pallas kernels, call(): pl.pallas_call(kernel, out_shape=[place(s, d) for s, d in outs], in_specs...  8.25 us
    ppermute x1, waiting for transfers between devices, step(): back_right = lax.ppermute(to_left, DOM, down)  7.01 us
    ppermute x1, starting transfers between devices, step(): from_left = lax.ppermute(own, DOM, up)  6.52 us
    all_gather x1, blocking collectives, step(): sums = lax.all_gather(half, 'c', axis=0, tiled=True)  5.2 us
    all_to_all x2, waiting for transfers between devices, swap(): return lax.all_to_all(x, axes, split_axis=0, concat_axis=0, tiled=True)  4.76 us
    ppermute x1, starting transfers between devices, step(): back_left = lax.ppermute(to_right, DOM, up)  3.76 us
  transfers between devices with their start and end apart: 6, of which 4 were waited for; matrix products, arithmetic and copies ran while one was open for 0% of the time, Pallas kernels for 2%

profile of v6, /device:TPU:63, one launch (start us, length us, event | category | flops | bytes accessed | tf_op | source)
XLA Modules:
  0.0 111.0 jit_solution(10597522854302436592)
XLA Ops:
  0.6 0.0 copy-start.1
  0.6 0.0 copy-start
  0.7 3.1 %collective-permute-start.1 = (bf16[128,256]{1,0:T(8,128)(2,1)}, bf16[128,256]{1,0:T(8,128)(2,1)S(1)}, u32[]{:S(2)}, u32[]{:S(2)}) collective-permute-start(bf16[128,256]{1,0:T(8,128)(2,1)} %bitcast.11), channel_id=1, source_target_pairs={{8,0},{16,8},{24,16},{32,24},{40,32},{48,40},{56,48},{64,56},{72,6... | collective-permute-start | bytes 196616 | tf_op jit(solution)/shard_map/ppermute | solution.py:297
  3.8 6.5 %collective-permute-start = (bf16[128,256]{1,0:T(8,128)(2,1)}, bf16[128,256]{1,0:T(8,128)(2,1)S(1)}, u32[]{:S(2)}, u32[]{:S(2)}) collective-permute-start(bf16[128,256]{1,0:T(8,128)(2,1)} %bitcast.12), channel_id=1, source_target_pairs={{0,8},{8,16},{16,24},{24,32},{32,40},{40,48},{48,56},{56,64},{64,7... | collective-permute-start | bytes 196616 | tf_op jit(solution)/shard_map/ppermute | solution.py:296
  10.3 1.3 %slots.1 = (bf16[2048,384]{1,0:T(8,128)(2,1)S(1)}, f32[128,16]{1,0:T(8,128)S(1)}, s32[16,128]{1,0:T(8,128)S(1)}, bf16[128,256]{1,0:T(8,128)(2,1)S(1)}, bf16[128,...) custom-call(s32[1]{0:T(128)} %bitcast.place, s32[16,128]{1,0:T(8,128)} %bitcast.15, ...), custom_call_target="tpu_custom_call" | custom-call | tf_op jit(solution)/shard_map/slots/pallas_call | solution.py:304
  11.6 0.0 collective-permute-done.1.right
  11.6 0.3 collective-permute-done.left
  11.9 1.4 %shard_map.119 = (bf16[128,256]{1,0:T(8,128)(2,1)S(1)}, bf16[8,2,16,256]{3,2,1,0:T(8,128)(2,1)S(1)}, bf16[2048,256]{1,0:T(8,128)(2,1)S(1)}) custom-call(bf16[128,256]{1,0:T(8,128)(2,1)S(1)} %collective-permute-done.left, bf16[128,256]{1,0:T(8,128)(2,1)S(1)} %get-tuple-element.30.own, bf16[128,256]{1,0:T(8,128)(2,1)S(1)} %collective-permute-done.1.right, ...), custom_call_target="tpu_custom_call" | custom-call | tf_op jit(solution)/shard_map/pallas_call | solution.py:38
  13.3 20.2 %all_to_all.25.got = bf16[8,2,16,256]{3,2,1,0:T(8,128)(2,1)S(1)} all-to-all(bf16[8,2,16,256]{3,2,1,0:T(8,128)(2,1)S(1)} %get-tuple-element.36), channel_id=1, replica_groups=mesh['zl'=2,'x'=4,'yh'=4,'yl'=2,'zh'=4,'c'=2] {'zh','c'}, dimensions={0} | all-to-all | bytes 262144 | tf_op jit(solution)/shard_map/all_to_all | solution.py:286
  33.6 0.0 copy-done.1
  33.6 0.0 copy-done
  33.6 2.0 %shard_map.120 = (bf16[8,16,256]{2,1,0:T(8,128)(2,1)}, bf16[128,256]{1,0:T(8,128)(2,1)S(1)}, bf16[3,128,256]{2,1,0:T(8,128)(2,1)S(1)}) custom-call(bf16[8,2,16,256]{3,2,1,0:T(8,128)(2,1)S(1)} %all_to_all.25.got, bf16[256,768]{1,0:T(8,128)(2,1)S(1)} %copy-done, bf16[256,256]{1,0:T(8,128)(2,1)S(1)} %copy-done.1), custom_call_target="tpu_custom_call" | custom-call | tf_op jit(solution)/shard_map/pallas_call | solution.py:38
  35.6 4.1 %all-to-all-start.1 = ((bf16[8,16,256]{2,1,0:T(8,128)(2,1)}), bf16[8,16,256]{2,1,0:T(8,128)(2,1)S(1)}, u32[]{:S(2)}, u32[]{:S(2)}) async-start(bf16[8,16,256]{2,1,0:T(8,128)(2,1)} %get-tuple-element.37), calls=%async_computation.1 | async-start | bytes 131072 | tf_op jit(solution)/shard_map/all_to_all | solution.py:286
  39.7 0.3 shard_map.123
  40.1 2.2 %all_gather.9.early_both = bf16[2,1024,128]{2,1,0:T(8,128)(2,1)S(1)} all-gather(bf16[1,1024,128]{2,1,0:T(8,128)(2,1)S(1)} %get-tuple-element.48), channel_id=1, replica_groups=mesh['zl'=2,'x'=4,'yh'=4,'yl'=2,'zh'=4,'c'=2] {'c'}, dimensions={0}, use_global_device_ids=true | all-gather | bytes 786432 | tf_op jit(solution)/shard_map/all_gather | solution.py:348
  42.2 4.8 %all-to-all-done.1 = bf16[8,16,256]{2,1,0:T(8,128)(2,1)S(1)} async-done(((bf16[8,16,256]{2,1,0:T(8,128)(2,1)}), bf16[8,16,256]{2,1,0:T(8,128)(2,1)S(1)}, u32[]{:S(2)}, u32[]{:S(2)}) %all-to-all-start.1) | async-done | bytes 65568 | tf_op jit(solution)/shard_map/all_to_all | solution.py:286
  47.0 1.5 %shard_map.121 = (bf16[128,256]{1,0:T(8,128)(2,1)S(1)}, bf16[128,256]{1,0:T(8,128)(2,1)S(1)}, f32[128,256]{1,0:T(8,128)S(1)}, f32[128,256]{1,0:T(8,128)S(1)}, bf...) custom-call(s32[1]{0:T(128)} %bitcast.place, bf16[128,256]{1,0:T(8,128)(2,1)S(1)} %bitcast.8, ...), custom_call_target="tpu_custom_call" | custom-call | tf_op jit(solution)/shard_map/pallas_call | solution.py:38
  48.5 2.6 %all_gather.10.late_both = bf16[2,512,128]{2,1,0:T(8,128)(2,1)S(1)} all-gather(bf16[1,512,128]{2,1,0:T(8,128)(2,1)S(1)} %get-tuple-element.50), channel_id=1, replica_groups=mesh['zl'=2,'x'=4,'yh'=4,'yl'=2,'zh'=4,'c'=2] {'c'}, dimensions={0}, use_global_device_ids=true | all-gather | bytes 393216 | tf_op jit(solution)/shard_map/all_gather | solution.py:368
  51.1 0.1 shard_map.124
  51.2 10.4 %all_to_all.26.parts = bf16[16,96,128]{2,1,0:T(8,128)(2,1)S(1)} all-to-all(bf16[16,96,128]{2,1,0:T(8,128)(2,1)S(1)} %shard_map.124), channel_id=1, replica_groups=mesh['zl'=2,'x'=4,'yh'=4,'yl'=2,'zh'=4,'c'=2] {'x','zl','yl'}, dimensions={0} | all-to-all | bytes 786432 | tf_op jit(solution)/shard_map/all_to_all | solution.py:286
  61.6 0.1 shard_map.125
  61.7 21.5 %all_to_all.27.parts = bf16[16,96,128]{2,1,0:T(8,128)(2,1)S(1)} all-to-all(bf16[16,96,128]{2,1,0:T(8,128)(2,1)S(1)} %shard_map.125), channel_id=1, replica_groups=mesh['zl'=2,'x'=4,'yh'=4,'yl'=2,'zh'=4,'c'=2] {'yh','zh'}, dimensions={0} | all-to-all | bytes 786432 | tf_op jit(solution)/shard_map/all_to_all | solution.py:286
  83.2 0.8 shard_map.126
  84.0 6.8 %all-to-all-start.4 = ((bf16[16,96,128]{2,1,0:T(8,128)(2,1)}), bf16[16,96,128]{2,1,0:T(8,128)(2,1)S(1)}, u32[]{:S(2)}, u32[]{:S(2)}) async-start(bf16[16,96,128]{2,1,0:T(8,128)(2,1)} %shard_map.126), calls=%async_computation.4 | async-start | bytes 786432 | tf_op jit(solution)/shard_map/all_to_all | solution.py:286
  90.7 3.8 %collective-permute-start.2 = (bf16[128,256]{1,0:T(8,128)(2,1)S(1)}, bf16[128,256]{1,0:T(8,128)(2,1)S(1)}, u32[]{:S(2)}, u32[]{:S(2)}) collective-permute-start(bf16[128,256]{1,0:T(8,128)(2,1)S(1)} %get-tuple-element.43), channel_id=1, source_target_pairs={{0,8},{8,16},{16,24},{24,32},{32,40},{40,48},{48,56},{56,64},{64,7... | collective-permute-start | bytes 196616 | tf_op jit(solution)/shard_map/ppermute | solution.py:363
  94.5 1.9 %collective-permute-start.3 = (bf16[128,256]{1,0:T(8,128)(2,1)S(1)}, bf16[128,256]{1,0:T(8,128)(2,1)S(1)}, u32[]{:S(2)}, u32[]{:S(2)}) collective-permute-start(bf16[128,256]{1,0:T(8,128)(2,1)S(1)} %get-tuple-element.44), channel_id=1, source_target_pairs={{8,0},{16,8},{24,16},{32,24},{40,32},{48,40},{56,48},{64,56},{72,6... | collective-permute-start | bytes 196616 | tf_op jit(solution)/shard_map/ppermute | solution.py:364
  96.4 0.3 collective-permute-done.2.from_left
  96.7 7.0 %collective-permute-done.3.from_right = bf16[128,256]{1,0:T(8,128)(2,1)S(1)} collective-permute-done((bf16[128,256]{1,0:T(8,128)(2,1)S(1)}, bf16[128,256]{1,0:T(8,128)(2,1)S(1)}, u32[]{:S(2)}, u32[]{:S(2)}) %collective-permute-start.3) | collective-permute-done | bytes 65568 | tf_op jit(solution)/shard_map/ppermute | solution.py:364
  103.7 0.8 shard_map.122
  104.6 0.0 all-to-all-done.4
  104.6 5.2 %all_gather.11.refs_0_ = bf16[2,1536,128]{2,1,0:T(8,128)(2,1)S(1)} all-gather(bf16[1,1536,128]{2,1,0:T(8,128)(2,1)S(1)} %bitcast.9), channel_id=1, replica_groups=mesh['zl'=2,'x'=4,'yh'=4,'yl'=2,'zh'=4,'c'=2] {'c'}, dimensions={0}, use_global_device_ids=true | all-gather | bytes 1179648 | tf_op jit(solution)/shard_map/all_gather | solution.py:378
  109.8 1.2 %shard_map.127 = (f32[256,256]{1,0:T(8,128)}, f32[256,256]{1,0:T(8,128)}, f32[256,768]{1,0:T(8,128)}, f32[256,256]{1,0:T(8,128)}) custom-call(bf16[2,1536,128]{2,1,0:T(8,128)(2,1)S(1)} %all_gather.11.refs_0_), custom_call_target="tpu_custom_call" | custom-call | tf_op jit(solution)/shard_map/pallas_call | solution.py:38
Async XLA Ops:
  0.6 32.9 %copy-start.1 = (bf16[256,256]{1,0:T(8,128)(2,1)S(1)}, bf16[256,256]{1,0:T(8,128)(2,1)}, u32[]{:S(2)}) copy-start(bf16[256,256]{1,0:T(8,128)(2,1)} %oproj.1) | copy-start | bytes 393220
  0.6 32.9 %copy-start = (bf16[256,768]{1,0:T(8,128)(2,1)S(1)}, bf16[256,768]{1,0:T(8,128)(2,1)}, u32[]{:S(2)}) copy-start(bf16[256,768]{1,0:T(8,128)(2,1)} %aproj.1) | copy-start | bytes 1179652
  0.7 10.9 %collective-permute-start.1 = (bf16[128,256]{1,0:T(8,128)(2,1)}, bf16[128,256]{1,0:T(8,128)(2,1)S(1)}, u32[]{:S(2)}, u32[]{:S(2)}) collective-permute-start(bf16[128,256]{1,0:T(8,128)(2,1)} %bitcast.11), channel_id=1, source_target_pairs={{8,0},{16,8},{24,16},{32,24},{40,32},{48,40},{56,48},{64,56},{72,6... | collective-permute-start | bytes 196616 | tf_op jit(solution)/shard_map/ppermute | solution.py:297
  3.8 8.2 %collective-permute-start = (bf16[128,256]{1,0:T(8,128)(2,1)}, bf16[128,256]{1,0:T(8,128)(2,1)S(1)}, u32[]{:S(2)}, u32[]{:S(2)}) collective-permute-start(bf16[128,256]{1,0:T(8,128)(2,1)} %bitcast.12), channel_id=1, source_target_pairs={{0,8},{8,16},{16,24},{24,32},{32,40},{40,48},{48,56},{56,64},{64,7... | collective-permute-start | bytes 196616 | tf_op jit(solution)/shard_map/ppermute | solution.py:296
  35.6 11.4 %all-to-all-start.1 = ((bf16[8,16,256]{2,1,0:T(8,128)(2,1)}), bf16[8,16,256]{2,1,0:T(8,128)(2,1)S(1)}, u32[]{:S(2)}, u32[]{:S(2)}) async-start(bf16[8,16,256]{2,1,0:T(8,128)(2,1)} %get-tuple-element.37), calls=%async_computation.1 | async-start | bytes 131072 | tf_op jit(solution)/shard_map/all_to_all | solution.py:286
  84.0 20.6 %all-to-all-start.4 = ((bf16[16,96,128]{2,1,0:T(8,128)(2,1)}), bf16[16,96,128]{2,1,0:T(8,128)(2,1)S(1)}, u32[]{:S(2)}, u32[]{:S(2)}) async-start(bf16[16,96,128]{2,1,0:T(8,128)(2,1)} %shard_map.126), calls=%async_computation.4 | async-start | bytes 786432 | tf_op jit(solution)/shard_map/all_to_all | solution.py:286
  90.7 6.0 %collective-permute-start.2 = (bf16[128,256]{1,0:T(8,128)(2,1)S(1)}, bf16[128,256]{1,0:T(8,128)(2,1)S(1)}, u32[]{:S(2)}, u32[]{:S(2)}) collective-permute-start(bf16[128,256]{1,0:T(8,128)(2,1)S(1)} %get-tuple-element.43), channel_id=1, source_target_pairs={{0,8},{8,16},{16,24},{24,32},{32,40},{40,48},{48,56},{56,64},{64,7... | collective-permute-start | bytes 196616 | tf_op jit(solution)/shard_map/ppermute | solution.py:363
  94.5 9.2 %collective-permute-start.3 = (bf16[128,256]{1,0:T(8,128)(2,1)S(1)}, bf16[128,256]{1,0:T(8,128)(2,1)S(1)}, u32[]{:S(2)}, u32[]{:S(2)}) collective-permute-start(bf16[128,256]{1,0:T(8,128)(2,1)S(1)} %get-tuple-element.44), channel_id=1, source_target_pairs={{8,0},{16,8},{24,16},{32,24},{40,32},{48,40},{56,48},{64,56},{72,6... | collective-permute-start | bytes 196616 | tf_op jit(solution)/shard_map/ppermute | solution.py:364
